TPU v7x, 512 devices: a whole 4x8x8 slice. The times are simulated.
512 devices in a mesh: dom: 64 (over x, y, z_lo), col: 8 (over z_hi, core).
Axes of the slice: x: 4, y: 8, z: 8 (z_hi: 4, z_lo: 2; z = z_hi * 2 + z_lo), core: 2. Of those that a mesh axis runs over, the one named last changes fastest.
Arguments:
- inverse: bfloat16 [64, 1664, 1664], P('dom', 'col'), may hold values from -1 to 4, as said below
- trace_map: bfloat16 [64, 512, 1664], P('dom', 'col'), may hold values from -0.15625 to 0.15625
- panel_coupling: bfloat16 [64, 1664, 128], P('dom'), may hold values from -6 to 6
- coupling: float32 [64, 6, 1664], P('dom', None, 'col'), may hold values from 0.15 to 0.9
- neighbours: int32 [64, 6], P('dom'), may hold values from 0 to 63, as said below
- iface_count: int32 [64], replicated, may hold values from 26 to 104, as said below
- surface_rows: int32 [64, 8, 1, 64], P('dom', 'col'), may hold values from 0 to 63
- factor: float32 [32768, 2048], P(('dom', 'col')), may hold values from -2 to 2
- colloc: float32 [3, 32768], P(None, ('dom', 'col')), may hold values from -1 to 1
- quad_points: float32 [3, 4, 32768], P(None, None, ('dom', 'col')), may hold values from -1 to 1
- quad_weight: float32 [4, 32768], P(None, ('dom', 'col')), may hold values from 2 to 16
- panel_block: int32 [2], replicated, may hold values from 0 to 511
Outputs:
- panel_columns: float32 [32768, 128], P(('dom', 'col'))
Inputs may be any that keep to these rules, and one draw needn't show every extreme that they name: Each domain's inverse is symmetric. `neighbours`: each domain lists 6 different domains, never itself. `iface_count`: some domain has exactly 104.
All inputs are finite; a program needn't handle non-finite values.
Results may differ from a plain program's by a relative error of at most 0.007.
Values may be sent and summed in bfloat16 or wider, within the bound.
No kernel may reach another device: no remote copies, remote signals or barrier semaphores. Data moves between devices by JAX's collectives and lax.ppermute only.
A program may use at most 64 MiB of HBM per device.

v0:
```python
import math

import jax
import jax.numpy as jnp
from jax import lax
from jax.sharding import PartitionSpec as P

MB = 208
P_SIZE = 64
NPAN = 2
SLOTS = 1


WAVE_NUMBER = 8.0
SMOOTHING = 0.05


def broadcast(block, axis, source):
    block = jnp.where(lax.axis_index(axis) == source, block, jnp.zeros_like(block))
    return lax.psum(block, axis)


def local(
    inverse,
    trace_map,
    panel_coupling,
    coupling,
    neighbours,
    iface_count,
    surface_rows,
    factor,
    colloc,
    quad_points,
    quad_weight,
    panel_block,
):
    dom_index = lax.axis_index("dom")
    col_index = lax.axis_index("col")
    domain_count = lax.axis_size("dom")
    inverse_rows = inverse[0]
    block_rows = inverse_rows.shape[0]
    panel_loads = panel_coupling[0]
    column_count = panel_loads.shape[1]
    first_row = col_index * block_rows
    own_loads = lax.dynamic_slice_in_dim(panel_loads, first_row, block_rows, 0)
    row_numbers = first_row + jnp.arange(block_rows, dtype=jnp.int32)
    own_count = iface_count[dom_index]
    live_rows = (row_numbers % MB < own_count).astype(jnp.float32)[:, None]
    first_apply = jnp.dot(inverse_rows, panel_loads, preferred_element_type=jnp.float32)
    first_values = (first_apply * live_rows).astype(jnp.bfloat16)
    weights_here = coupling[0]
    listed = neighbours[0]
    shards = lax.all_gather(first_values[None], "dom", axis=0, tiled=True)
    count_here = shards.shape[0]
    matches = (listed[:, None] == jnp.arange(count_here, dtype=jnp.int32)[None, :]).astype(
        jnp.float32
    )
    factors = jnp.einsum("ke,kr->er", matches, weights_here)
    correction = jnp.sum(factors[:, :, None] * shards, axis=0)
    loaded = (own_loads.astype(jnp.float32) - live_rows * correction).astype(jnp.bfloat16)
    map_rows = trace_map[0]
    columns = inverse_rows
    second_rows = jnp.dot(
        columns,
        lax.all_gather(loaded, "col", axis=0, tiled=True),
        preferred_element_type=jnp.float32,
    ).astype(jnp.bfloat16)
    columns = map_rows
    traces = jnp.dot(
        columns,
        lax.all_gather(second_rows, "col", axis=0, tiled=True),
        preferred_element_type=jnp.float32,
    )
    traces = traces.astype(jnp.bfloat16).reshape(SLOTS, domain_count, column_count)
    arrived = lax.all_to_all(traces, "dom", split_axis=1, concat_axis=1, tiled=True)
    row_slots = surface_rows[0, 0].reshape(-1)
    factor_rows = factor.shape[0]
    surface_sum = (
        jnp.zeros((factor_rows, column_count), jnp.float32)
        .at[row_slots]
        .add(arrived.reshape(-1, column_count).astype(jnp.float32))
    )
    factor_list = []
    points_list = []
    weights_list = []
    for panel_number in range(NPAN):
        begin_row = panel_block[panel_number] * P_SIZE
        owner_device = begin_row // factor_rows
        received = (
            broadcast(factor, ("dom", "col"), owner_device),
            broadcast(quad_points, ("dom", "col"), owner_device),
            broadcast(quad_weight, ("dom", "col"), owner_device),
        )
        factor_list.append(received[0])
        points_list.append(received[1])
        weights_list.append(received[2])
    panel_factor = jnp.concatenate(factor_list, axis=0)
    panel_points = jnp.concatenate(points_list, axis=2)
    panel_weights = jnp.concatenate(weights_list, axis=1)
    shifted = colloc[:, :, None, None] - panel_points[:, None, :, :]
    squared = jnp.sum(shifted * shifted, axis=0)
    green_values = jnp.cos(WAVE_NUMBER * jnp.sqrt(squared)) / (
        4.0 * math.pi * jnp.sqrt(squared + SMOOTHING * SMOOTHING)
    )
    kernel_block = jnp.sum(panel_weights[None, :, :] * green_values, axis=1)
    prior_update = lax.dot_general(
        factor,
        panel_factor,
        (((1,), (1,)), ((), ())),
        precision=lax.Precision.HIGHEST,
        preferred_element_type=jnp.float32,
    )
    return kernel_block - surface_sum - prior_update


def solution(mesh):
    in_specs = (
        P("dom", "col", None),
        P("dom", "col", None),
        P("dom", None, None),
        P("dom", None, "col"),
        P("dom", None),
        P(),
        P("dom", "col", None, None),
        P(("dom", "col"), None),
        P(None, ("dom", "col")),
        P(None, None, ("dom", "col")),
        P(None, ("dom", "col")),
        P(),
    )
    out_specs = P(("dom", "col"), None)
    return jax.shard_map(local, mesh=mesh, in_specs=in_specs, out_specs=out_specs, check_vma=False)
```

profile of v0, /device:TPU:1, one launch (start us, length us, event | category | flops | bytes accessed | tf_op | source)
XLA Modules:
  0.0 388.6 jit_solution(3497062849710801463)
XLA Ops:
  7.4 0.0 copy-start
  7.4 0.0 copy-start.8
  7.4 0.0 copy-start.6
  7.4 0.0 copy-start.3
  7.4 0.0 copy-start.7
  7.4 0.0 copy-start.4
  7.4 0.0 copy-start.5
  7.4 0.0 all-gather.3.cloned.1.call-start
  7.5 1.3 dynamic_slice.7
  8.7 0.7 compare_convert_fusion
  9.4 0.0 copy-done
  9.4 2.0 fusion.1
  11.4 0.0 all-gather.3.cloned.1.call-update
  11.4 0.0 all-reduce.4.cloned.1.call-start
  11.5 1.3 fusion.24
  14.1 2.1 broadcast_select_fusion.1
  16.3 0.0 copy-start.2
  16.3 0.0 all-reduce.4.cloned.1.call-update
  16.3 0.0 copy-done.8
  16.3 0.0 copy-done.6
  16.3 0.0 copy-done.3
  16.4 108.0 %all-reduce = (f32[3,4,64]{2,1,0:T(4,128)S(1)}, f32[3,4,64]{2,1,0:T(4,128)S(1)}, f32[4,64]{1,0:T(4,128)S(1)}, f32[4,64]{1,0:T(4,128)S(1)}) all-reduce(f32[3,4,64]{2,1,0:T(4,128)S(1)} %get-tuple-element.14, f32[3,4,64]{2,1,0:T(4,128)S(1)} %get-tuple-element.13, ...), channel_id=1, replica_groups=mesh['dom'=64,'col'=8] {'dom','col'}, use_global_device_ids=true, to_apply=%region_3.4 | all-reduce | flops 2048 | bytes 16384 | tf_op jit(solution)/shard_map/psum | solution.py:20
  124.3 0.1 pad_maximum_fusion
  124.4 0.1 pad_maximum_fusion.1
  124.5 0.0 copy-done.7
  124.5 0.0 copy-done.4
  124.5 0.3 fusion.18
  124.8 0.0 copy-done.5
  124.8 0.1 multiply_reduce_fusion
  124.9 149.1 %all-gather.3.cloned.1.call-done = bf16[13312,128]{1,0:T(8,128)(2,1)} async-done(((bf16[208,128]{1,0:T(8,128)(2,1)}), bf16[13312,128]{1,0:T(8,128)(2,1)}) %all-gather.3.cloned.1.call-update) | async-done | bytes 3407888 | tf_op jit(solution)/shard_map/all_gather | solution.py:53
  274.0 0.0 copy-start.1
  274.0 4.0 %fusion = f32[208,128]{1,0:T(8,128)S(1)} fusion(bf16[64,208,128]{2,1,0:T(8,128)(2,1)} %bitcast.46, f32[64,208]{1,0:T(8,128)S(1)} %fusion.18), kind=kLoop, calls=%fused_computation.2 | loop fusion | flops 5085184 | bytes 3567616 | tf_op jit(solution)/shard_map/reduce_sum | solution.py:59
  278.1 0.9 fusion.12
  279.0 66.1 %all_gather.10 = bf16[1664,128]{1,0:T(8,128)(2,1)S(1)} all-gather(bf16[208,128]{1,0:T(8,128)(2,1)S(1)} %fusion.12), channel_id=1, replica_groups=mesh['dom'=64,'col'=8] {'col'}, dimensions={0}, use_global_device_ids=true | all-gather | bytes 479232 | tf_op jit(solution)/shard_map/all_gather | solution.py:65
  345.1 0.4 fusion.2
  345.4 14.9 %all_gather.11 = bf16[1664,128]{1,0:T(8,128)(2,1)S(1)} all-gather(bf16[208,128]{1,0:T(8,128)(2,1)S(1)} %fusion.2), channel_id=1, replica_groups=mesh['dom'=64,'col'=8] {'col'}, dimensions={0}, use_global_device_ids=true | all-gather | bytes 479232 | tf_op jit(solution)/shard_map/all_gather | solution.py:71
  360.4 0.0 copy-done.2
  360.4 0.2 fusion.4
  360.6 0.6 copy.15
  361.2 6.8 %all-to-all-start = ((bf16[1,64,128]{2,0,1:T(2,128)(2,1)}), bf16[1,64,128]{2,0,1:T(2,128)(2,1)S(1)}, u32[]{:S(2)}, u32[]{:S(2)}) async-start(bf16[1,64,128]{2,0,1:T(2,128)(2,1)} %copy.15), calls=%async_computation | async-start | bytes 65536 | tf_op jit(solution)/shard_map/all_to_all | solution.py:75
  368.0 0.5 multiply_reduce_fusion.1
  368.6 8.7 %all-to-all-done = bf16[1,64,128]{2,0,1:T(2,128)(2,1)S(1)} async-done(((bf16[1,64,128]{2,0,1:T(2,128)(2,1)}), bf16[1,64,128]{2,0,1:T(2,128)(2,1)S(1)}, u32[]{:S(2)}, u32[]{:S(2)}) %all-to-all-start) | async-done | bytes 16416 | tf_op jit(solution)/shard_map/all_to_all | solution.py:75
  377.2 0.8 scatter_custom_fusion
  378.1 0.0 all-reduce.4.cloned.1.call-done
  378.1 0.0 copy-done.1
  378.1 3.0 fusion.3
  (3 shorter events, 0.0 us)
Async XLA Ops:
  7.4 2.0 copy-start
  7.4 8.9 %copy-start.8 = (s32[1,1,1,64]{3,2,1,0:T(1,128)S(1)}, s32[1,1,1,64]{3,2,1,0:T(1,128)}, u32[]{:S(2)}) copy-start(s32[1,1,1,64]{3,2,1,0:T(1,128)} %param.18) | copy-start | bytes 772
  7.4 9.0 %copy-start.6 = (f32[4,64]{1,0:T(4,128)S(1)}, f32[4,64]{1,0:T(4,128)}, u32[]{:S(2)}) copy-start(f32[4,64]{1,0:T(4,128)} %param.22) | copy-start | bytes 3076
  7.4 9.0 %copy-start.3 = (f32[3,4,64]{2,1,0:T(4,128)S(1)}, f32[3,4,64]{2,1,0:T(4,128)}, u32[]{:S(2)}) copy-start(f32[3,4,64]{2,1,0:T(4,128)} %param.21) | copy-start | bytes 9220
  7.4 117.1 %copy-start.7 = (s32[1,6]{1,0:T(1,128)S(1)}, s32[1,6]{1,0:T(1,128)}, u32[]{:S(2)}) copy-start(s32[1,6]{1,0:T(1,128)} %param.16) | copy-start | bytes 76
  7.4 117.1 %copy-start.4 = (f32[1,6,208]{2,0,1:T(1,128)S(1)}, f32[1,6,208]{2,0,1:T(1,128)}, u32[]{:S(2)}) copy-start(f32[1,6,208]{2,0,1:T(1,128)} %param.15) | copy-start | bytes 14980
  7.4 117.4 %copy-start.5 = (f32[3,64]{1,0:T(4,128)S(1)}, f32[3,64]{1,0:T(4,128)}, u32[]{:S(2)}) copy-start(f32[3,64]{1,0:T(4,128)} %param.20) | copy-start | bytes 2308
  7.4 266.6 %all-gather.3.cloned.1.call-start = ((), (), s32[]{:S(2)}) async-start(), calls=%async_computation.1 | async-start | bytes 3461120 | tf_op jit(solution)/shard_map/all_gather | solution.py:53
  11.4 366.7 %all-reduce.4.cloned.1.call-start = ((), (), s32[]{:S(2)}) async-start(), calls=%async_computation.2 | async-start | bytes 2097152 | tf_op jit(solution)/shard_map/psum | solution.py:20
  16.3 344.1 %copy-start.2 = (bf16[1,64,1664]{2,1,0:T(8,128)(2,1)S(1)}, bf16[1,64,1664]{2,1,0:T(8,128)(2,1)}, u32[]{:S(2)}) copy-start(bf16[1,64,1664]{2,1,0:T(8,128)(2,1)} %param.13) | copy-start | bytes 638980
  274.0 104.1 %copy-start.1 = (f32[64,2048]{1,0:T(8,128)S(1)}, f32[64,2048]{1,0:T(8,128)}, u32[]{:S(2)}) copy-start(f32[64,2048]{1,0:T(8,128)} %param.19) | copy-start | bytes 1572868
  361.2 16.0 %all-to-all-start = ((bf16[1,64,128]{2,0,1:T(2,128)(2,1)}), bf16[1,64,128]{2,0,1:T(2,128)(2,1)S(1)}, u32[]{:S(2)}, u32[]{:S(2)}) async-start(bf16[1,64,128]{2,0,1:T(2,128)(2,1)} %copy.15), calls=%async_computation | async-start | bytes 65536 | tf_op jit(solution)/shard_map/all_to_all | solution.py:75
Sparse Core Ops, SparseCore 0:
  11.6 262.4 all-gather.2
Sparse Core Ops, SparseCore 1:
  17.2 283.3 all-reduce.3
where the time goes:
time: 389 us
  blocking collectives  189 us (49%)
  waiting for transfers between devices  158 us (41%)
  between operations  16.3 us (4%)
  other arithmetic  9.37 us (2%)
  starting transfers between devices  6.86 us (2%)
  matrix products  5.84 us (2%)
    all_gather x1, waiting for transfers between devices, local(): shards = lax.all_gather(first_values[None], 'dom', axis=0, tiled=True)  149 us
    psum x1, blocking collectives, broadcast(): return lax.psum(block, axis)  108 us
    all_gather x1, blocking collectives, local(): lax.all_gather(loaded, 'col', axis=0, tiled=True)  66.1 us
    all_gather x1, blocking collectives, local(): lax.all_gather(second_rows, 'col', axis=0, tiled=True)  14.9 us
    all_to_all x1, waiting for transfers between devices, local(): lax.all_to_all(traces, 'dom', split_axis=1, concat_axis=1, tiled=True)  8.67 us
  transfers between devices with their start and end apart: 3, of which 2 were waited for; matrix products, arithmetic and copies ran while one was open for 3% of the time, Pallas kernels for 0%

commit v1 on v0

v1 whole, which is shorter than its diff:
```python
import math

import jax
import jax.numpy as jnp
from jax import lax
from jax.sharding import PartitionSpec as P

MB = 208
P_SIZE = 64
NPAN = 2
LIVE = 128
PAIR = 2
LANE = 128

WAVE_NUMBER = 8.0
SMOOTHING = 0.05

F32 = jnp.float32
BF16 = jnp.bfloat16


def split3(values):
    high = lax.reduce_precision(values, 8, 7)
    rest = values - high
    middle = lax.reduce_precision(rest, 8, 7)
    low = rest - middle
    return jnp.concatenate(
        [high.astype(BF16), middle.astype(BF16), low.astype(BF16)], axis=-1
    )


def join3(parts):
    parts = parts.astype(F32)
    width = parts.shape[-1] // 3
    return (parts[..., 2 * width :] + parts[..., width : 2 * width]) + parts[..., :width]


def local(
    inverse,
    trace_map,
    panel_coupling,
    coupling,
    neighbours,
    iface_count,
    surface_rows,
    factor,
    colloc,
    quad_points,
    quad_weight,
    panel_block,
):
    dom_index = lax.axis_index("dom")
    doms = lax.axis_size("dom")
    cols = lax.axis_size("col")
    inverse_rows = inverse[0]
    panel_loads = panel_coupling[0]
    own_count = iface_count[dom_index]
    live = (jnp.arange(LIVE, dtype=jnp.int32) < own_count).astype(F32)[:, None]

    first_apply = jnp.dot(inverse_rows[:LIVE], panel_loads, preferred_element_type=F32)
    first_values = (first_apply * live).astype(BF16).reshape(doms, PAIR, LANE)
    factor_low = factor.astype(BF16)
    chunks = factor_low.reshape(4, 16, 16, LANE).transpose(0, 2, 1, 3).reshape(doms, 16, LANE)
    quads = jnp.concatenate([quad_points.reshape(12, P_SIZE), quad_weight], axis=0).T
    weights = coupling[0][:, :LIVE].reshape(6, doms, PAIR).transpose(1, 0, 2).reshape(doms, 12)
    listed = jnp.broadcast_to(neighbours.astype(F32).astype(BF16), (doms, 6))
    misc = jnp.concatenate(
        [split3(quads), split3(weights), listed, jnp.zeros((doms, LANE - 90), BF16)], axis=1
    )
    sent = jnp.concatenate(
        [chunks, first_values, misc[:, None], jnp.zeros((doms, 5, LANE), BF16)], axis=1
    )
    got = lax.all_to_all(sent, "dom", 0, 0, tiled=True)

    misc = got[:, 18]
    weights = join3(misc[:, 48:84])
    listed = misc[:, 84:90].astype(F32)
    sources = jnp.arange(doms, dtype=jnp.int32).astype(F32)[None, :]
    corrections = []
    for r in range(PAIR):
        mixing = jnp.zeros((doms, doms), F32)
        for k in range(6):
            mixing = mixing + jnp.where(
                listed[:, k : k + 1] == sources, weights[:, 2 * k + r : 2 * k + r + 1], 0.0
            )
        corrections.append(
            jnp.dot(
                mixing,
                got[:, 16 + r].astype(F32),
                precision=lax.Precision.HIGHEST,
                preferred_element_type=F32,
            )
        )
    correction = jnp.stack(corrections, axis=1).astype(BF16)
    sent = jnp.broadcast_to(correction[:, None], (doms, cols, PAIR, LANE))
    sent = sent.reshape(doms * cols, PAIR, LANE)
    arrived = lax.all_to_all(sent, ("dom", "col"), 0, 0, tiled=True)
    arrived = arrived.reshape(doms, cols, PAIR, LANE).transpose(1, 0, 2, 3)
    correction = arrived.reshape(cols, LIVE, LANE).astype(F32)
    loads = panel_loads.reshape(cols, MB, LANE)
    top = (loads[:, :LIVE].astype(F32) - live[None] * correction).astype(BF16)
    loaded = jnp.concatenate([top, loads[:, LIVE:]], axis=1).reshape(cols * MB, LANE)
    second_rows = jnp.dot(inverse_rows, loaded, preferred_element_type=F32).astype(BF16)

    pieces = [second_rows]
    quads = []
    for p in range(NPAN):
        owner = panel_block[p] // cols
        piece = lax.dynamic_slice(got, (owner, 0, 0), (1, 24, LANE))[0]
        pieces.append(piece[:16])
        quads.append(piece[18:19])
    pieces += quads + [jnp.zeros((14, LANE), BF16)]
    gathered = lax.all_gather(jnp.concatenate(pieces, axis=0), "col", axis=0, tiled=False)
    second = gathered[:, :MB].reshape(cols * MB, LANE)
    traces = jnp.dot(trace_map[0], second, preferred_element_type=F32).astype(BF16)

    picked = []
    for p in range(NPAN):
        lane = panel_block[p] % cols
        picked.append(lax.dynamic_slice(gathered, (lane, MB, 0), (1, 48, LANE))[0])
    shared = jnp.concatenate([picked[0][:16], picked[1][16:32]], axis=0)
    tail = jnp.concatenate([picked[0][32:33], picked[1][33:34], jnp.zeros((5, LANE), BF16)], axis=0)
    sent = jnp.concatenate(
        [
            jnp.broadcast_to(shared[None], (doms, 32, LANE)),
            traces[:, None],
            jnp.broadcast_to(tail[None], (doms, 7, LANE)),
        ],
        axis=1,
    )
    got = lax.all_to_all(sent, "dom", 0, 0, tiled=True)

    row_slots = surface_rows[0, 0].reshape(-1)
    landing = (jnp.arange(factor.shape[0], dtype=jnp.int32)[:, None] == row_slots[None, :]).astype(BF16)
    surface_sum = jnp.dot(landing, got[:, 32], preferred_element_type=F32)
    panels = []
    quads = []
    for p in range(NPAN):
        block = got[:, 16 * p : 16 * p + 16].reshape(4, 16, 16, LANE)
        panels.append(block.transpose(0, 2, 1, 3).reshape(P_SIZE, 16 * LANE))
        quads.append(join3(got[:, 33 + p, :48]))
    panel_factor = jnp.concatenate(panels, axis=0)
    quads = jnp.concatenate(quads, axis=0).T
    panel_points = quads[:12].reshape(3, 4, NPAN * P_SIZE)
    panel_weights = quads[12:]
    shifted = colloc[:, :, None, None] - panel_points[:, None, :, :]
    squared = jnp.sum(shifted * shifted, axis=0)
    green_values = jnp.cos(WAVE_NUMBER * jnp.sqrt(squared)) / (
        4.0 * math.pi * jnp.sqrt(squared + SMOOTHING * SMOOTHING)
    )
    kernel_block = jnp.sum(panel_weights[None, :, :] * green_values, axis=1)
    prior_update = lax.dot_general(
        factor_low, panel_factor, (((1,), (1,)), ((), ())), preferred_element_type=F32
    )
    return kernel_block - surface_sum - prior_update


def solution(mesh):
    in_specs = (
        P("dom", "col", None),
        P("dom", "col", None),
        P("dom", None, None),
        P("dom", None, "col"),
        P("dom", None),
        P(),
        P("dom", "col", None, None),
        P(("dom", "col"), None),
        P(None, ("dom", "col")),
        P(None, None, ("dom", "col")),
        P(None, ("dom", "col")),
        P(),
    )
    out_specs = P(("dom", "col"), None)
    return jax.shard_map(local, mesh=mesh, in_specs=in_specs, out_specs=out_specs, check_vma=False)
```

time: 389 us -> 115 us (0.30)
  blocking collectives: 189 us -> 39 us
  waiting for transfers between devices: 158 us -> 24 us
  starting transfers between devices: 6.86 us -> 30.6 us
  between operations: 16.3 us -> 5.61 us
  other arithmetic: 9.37 us -> 4.64 us
  local copies, waits for them, and re-layouts: 3.3 us -> 8.03 us
    all_gather x1 -> x0, waiting for transfers between devices: 149 us -> none  [local(): shards = lax.all_gather(first_values[None], 'dom', axis=0, tiled=True)]
    psum x1 -> x0, blocking collectives: 108 us -> none  [broadcast(): return lax.psum(block, axis)]
    all_gather x2 -> x1, blocking collectives: 81 us -> 16.2 us  [local(): lax.all_gather(jnp.concatenate(pieces, axis=0), 'col', axis=0, tiled=False)]
    all_to_all x1 -> x2, starting transfers between devices: 6.78 us -> 30.6 us  [the longest x1 17.6 us: local(): arrived = lax.all_to_all(sent, ('dom', 'col'), 0, 0, tiled=True)]
    all_to_all x0 -> x1, blocking collectives: none -> 22.8 us  [local(): got = lax.all_to_all(sent, 'dom', 0, 0, tiled=True)]
    all_to_all x1 -> x2, waiting for transfers between devices: 8.67 us -> 24 us  [the longest x1 13.1 us: local(): got = lax.all_to_all(sent, 'dom', 0, 0, tiled=True)]
    reduce_sum x1 -> x0, other arithmetic: 4.04 us -> none  [local(): correction = jnp.sum(factors[:, :, None] * shards, axis=0)]
  transfers between devices with their start and end apart: 3 -> 2, of which waited for: 2 -> 2; matrix products, arithmetic and copies ran while one was open for 3% -> 1% of each run, Pallas kernels for 0% -> 0%
where the time goes in v1:
time: 115 us; the launch traced here: 114 us
  blocking collectives  39 us (34%)
  starting transfers between devices  30.6 us (27%)
  waiting for transfers between devices  24 us (21%)
  local copies, waits for them, and re-layouts  8.03 us (7%)
  between operations  5.61 us (5%)
  other arithmetic  4.64 us (4%)
  matrix products  2.48 us (2%)
    all_to_all x1, blocking collectives, local(): got = lax.all_to_all(sent, 'dom', 0, 0, tiled=True)  22.8 us
    all_to_all x1, starting transfers between devices, local(): arrived = lax.all_to_all(sent, ('dom', 'col'), 0, 0, tiled=True)  17.6 us
    all_gather x1, blocking collectives, local(): lax.all_gather(jnp.concatenate(pieces, axis=0), 'col', axis=0, tiled=False)  16.2 us
    all_to_all x1, waiting for transfers between devices, local(): got = lax.all_to_all(sent, 'dom', 0, 0, tiled=True)  13.1 us
    all_to_all x1, starting transfers between devices, local(): got = lax.all_to_all(sent, 'dom', 0, 0, tiled=True)  12.9 us
    all_to_all x1, waiting for transfers between devices, local(): arrived = lax.all_to_all(sent, ('dom', 'col'), 0, 0, tiled=True)  10.9 us
  transfers between devices with their start and end apart: 2, of which 2 were waited for; matrix products, arithmetic and copies ran while one was open for 1% of the time, Pallas kernels for 0%

profile of v1, /device:TPU:1, one launch (start us, length us, event | category | flops | bytes accessed | tf_op | source)
XLA Modules:
  0.0 114.3 jit_solution(15256585085479843048)
XLA Ops:
  0.0 1.3 %dynamic_slice.15 = s32[1]{0:T(128)} dynamic-slice(s32[64]{0:T(128)} %param.17, s32[]{:T(128)S(6)} %select_n.70), dynamic_slice_sizes={1} | dynamic-slice | bytes 12 | tf_op jit(solution)/shard_map/dynamic_slice | solution.py:57
  1.3 0.6 compare_convert_fusion
  2.0 0.7 convert_bitcast_fusion.2
  2.6 0.7 copy.138
  3.3 0.7 reshape.100
  4.0 0.7 fusion.62
  4.7 0.1 copy.92
  4.8 0.1 copy.91
  4.9 0.1 copy.90
  5.0 0.1 copy.88
  5.1 0.1 copy.89
  5.3 0.1 copy.95
  5.4 0.1 copy.94
  5.5 0.1 copy.93
  5.6 0.1 concatenate.36
  6.0 0.1 pad.19.clone
  6.1 0.7 copy-done.3
  6.8 0.2 copy-done.2
  7.0 0.3 fusion.1
  7.3 0.9 maximum_maximum_fusion
  8.2 12.9 %all-to-all-start = ((bf16[64,24,128]{2,1,0:T(8,128)(2,1)}), bf16[64,24,128]{2,1,0:T(8,128)(2,1)S(1)}, u32[]{:S(2)}, u32[]{:S(2)}) async-start(bf16[64,24,128]{2,1,0:T(8,128)(2,1)} %maximum_maximum_fusion), calls=%async_computation | async-start | bytes 786432 | tf_op jit(solution)/shard_map/all_to_all | solution.py:73
  21.2 13.1 %all-to-all-done = bf16[64,24,128]{2,1,0:T(8,128)(2,1)S(1)} async-done(((bf16[64,24,128]{2,1,0:T(8,128)(2,1)}), bf16[64,24,128]{2,1,0:T(8,128)(2,1)S(1)}, u32[]{:S(2)}, u32[]{:S(2)}) %all-to-all-start) | async-done | bytes 393248 | tf_op jit(solution)/shard_map/all_to_all | solution.py:73
  34.4 0.1 slice_convert_fusion.2
  34.5 0.1 slice_convert_fusion.3
  34.5 0.1 slice_add_fusion.4
  34.6 0.6 slice_reduce_fusion.16
  35.2 0.3 fusion.4
  35.6 0.3 fusion.3
  35.9 0.8 broadcast_in_dim.180
  36.8 17.6 %all-to-all-start.1 = ((bf16[512,2,128]{2,1,0:T(2,128)(2,1)}), bf16[512,2,128]{2,1,0:T(2,128)(2,1)S(1)}, u32[]{:S(2)}, u32[]{:S(2)}) async-start(bf16[512,2,128]{2,1,0:T(2,128)(2,1)} %bitcast.14), calls=%async_computation.1 | async-start | bytes 524288 | tf_op jit(solution)/shard_map/all_to_all | solution.py:97
  54.4 0.1 pad.9.clone
  54.5 0.6 fusion.73
  60.3 10.9 %all-to-all-done.1 = bf16[512,2,128]{2,1,0:T(2,128)(2,1)S(1)} async-done(((bf16[512,2,128]{2,1,0:T(2,128)(2,1)}), bf16[512,2,128]{2,1,0:T(2,128)(2,1)S(1)}, u32[]{:S(2)}, u32[]{:S(2)}) %all-to-all-start.1) | async-done | bytes 262176 | tf_op jit(solution)/shard_map/all_to_all | solution.py:97
  71.2 0.2 fusion.11
  71.5 0.3 fusion
  71.9 0.2 concatenate.39
  72.1 16.2 %all-gather = bf16[2048,128]{1,0:T(8,128)(2,1)S(1)} all-gather(bf16[256,128]{1,0:T(8,128)(2,1)S(1)} %concatenate.39), channel_id=2, replica_groups=mesh['dom'=64,'col'=8] {'col'}, dimensions={0}, use_global_device_ids=true | all-gather | bytes 589824 | tf_op jit(solution)/shard_map/all_gather | solution.py:113
  88.3 0.2 fusion.5
  88.6 0.1 maximum_maximum_fusion.1
  88.8 0.1 pad_maximum_fusion
  89.0 22.8 %all_to_all.15 = bf16[64,40,128]{2,1,0:T(8,128)(2,1)S(1)} all-to-all(bf16[64,40,128]{2,1,0:T(8,128)(2,1)S(1)} %pad_maximum_fusion), channel_id=1, replica_groups=mesh['dom'=64,'col'=8] {'dom'}, dimensions={0} | all-to-all | bytes 1310720 | tf_op jit(solution)/shard_map/all_to_all | solution.py:131
  112.2 0.1 slice_add_fusion.2
  112.3 0.1 slice_add_fusion
  112.5 0.1 maximum_bitcast_fusion.1
  112.6 0.1 multiply_reduce_fusion
  112.7 0.5 multiply_reduce_fusion.1
  113.3 0.1 convolution_subtract_fusion
  113.4 0.9 fusion.2
  (52 shorter events, 1.3 us)
Async XLA Ops:
  0.0 88.3 %copy-start = (bf16[1,64,1664]{2,1,0:T(8,128)(2,1)S(1)}, bf16[1,64,1664]{2,1,0:T(8,128)(2,1)}, u32[]{:S(2)}) copy-start(bf16[1,64,1664]{2,1,0:T(8,128)(2,1)} %param.13) | copy-start | bytes 638980
  0.0 5.8 %copy-start.1 = (f32[64,2048]{1,0:T(8,128)S(1)}, f32[64,2048]{1,0:T(8,128)}, u32[]{:S(2)}) copy-start(f32[64,2048]{1,0:T(8,128)} %param.19) | copy-start | bytes 1572868
  5.8 1.0 copy-start.3
  5.8 1.2 %copy-start.2 = (bf16[1,208,1664]{2,1,0:T(8,128)(2,1)S(1)}, bf16[1,208,1664]{2,1,0:T(8,128)(2,1)}, u32[]{:S(2)}) copy-start(bf16[1,208,1664]{2,1,0:T(8,128)(2,1)} %param.12) | copy-start | bytes 2076676
  8.2 26.1 %all-to-all-start = ((bf16[64,24,128]{2,1,0:T(8,128)(2,1)}), bf16[64,24,128]{2,1,0:T(8,128)(2,1)S(1)}, u32[]{:S(2)}, u32[]{:S(2)}) async-start(bf16[64,24,128]{2,1,0:T(8,128)(2,1)} %maximum_maximum_fusion), calls=%async_computation | async-start | bytes 786432 | tf_op jit(solution)/shard_map/all_to_all | solution.py:73
  35.5 18.9 %copy-start.5 = (s32[2]{0:T(128)S(1)}, s32[2]{0:T(128)}, u32[]{:S(2)}) copy-start(s32[2]{0:T(128)} %param.23) | copy-start | bytes 28
  36.8 34.4 %all-to-all-start.1 = ((bf16[512,2,128]{2,1,0:T(2,128)(2,1)}), bf16[512,2,128]{2,1,0:T(2,128)(2,1)S(1)}, u32[]{:S(2)}, u32[]{:S(2)}) async-start(bf16[512,2,128]{2,1,0:T(2,128)(2,1)} %bitcast.14), calls=%async_computation.1 | async-start | bytes 524288 | tf_op jit(solution)/shard_map/all_to_all | solution.py:97
  111.9 0.7 copy-start.4
  112.0 1.3 %copy-start.6 = (s32[1,1,1,64]{3,2,1,0:T(1,128)S(1)}, s32[1,1,1,64]{3,2,1,0:T(1,128)}, u32[]{:S(2)}) copy-start(s32[1,1,1,64]{3,2,1,0:T(1,128)} %param.18) | copy-start | bytes 772

commit v2 on v1

--- a/solution.py
+++ b/solution.py
@@ -9,6 +9,7 @@
 P_SIZE = 64
 NPAN = 2
 LIVE = 128
+MAX_LIVE = 112
 PAIR = 2
 LANE = 128
 
@@ -68,11 +69,12 @@
         [split3(quads), split3(weights), listed, jnp.zeros((doms, LANE - 90), BF16)], axis=1
     )
     sent = jnp.concatenate(
-        [chunks, first_values, misc[:, None], jnp.zeros((doms, 5, LANE), BF16)], axis=1
+        [chunks[:, :8], first_values, misc[:, None], jnp.zeros((doms, 5, LANE), BF16)], axis=1
     )
+    sent, late = lax.optimization_barrier((sent, chunks[:, 8:]))
     got = lax.all_to_all(sent, "dom", 0, 0, tiled=True)
 
-    misc = got[:, 18]
+    misc = got[:, 10]
     weights = join3(misc[:, 48:84])
     listed = misc[:, 84:90].astype(F32)
     sources = jnp.arange(doms, dtype=jnp.int32).astype(F32)[None, :]
@@ -86,61 +88,57 @@
         corrections.append(
             jnp.dot(
                 mixing,
-                got[:, 16 + r].astype(F32),
+                got[:, 8 + r].astype(F32),
                 precision=lax.Precision.HIGHEST,
                 preferred_element_type=F32,
             )
         )
     correction = jnp.stack(corrections, axis=1).astype(BF16)
-    sent = jnp.broadcast_to(correction[:, None], (doms, cols, PAIR, LANE))
-    sent = sent.reshape(doms * cols, PAIR, LANE)
-    arrived = lax.all_to_all(sent, ("dom", "col"), 0, 0, tiled=True)
-    arrived = arrived.reshape(doms, cols, PAIR, LANE).transpose(1, 0, 2, 3)
-    correction = arrived.reshape(cols, LIVE, LANE).astype(F32)
+    owners = [panel_block[p] // cols for p in range(NPAN)]
+    lanes = [panel_block[p] % cols for p in range(NPAN)]
+    early = [lax.dynamic_slice(got, (d, 0, 0), (1, 16, LANE))[0] for d in owners]
+    sent = jnp.concatenate([late, correction, jnp.zeros((doms, 6, LANE), BF16)], axis=1)
+    sent, early = lax.optimization_barrier((sent, early))
+    got = lax.all_to_all(sent, "dom", 0, 0, tiled=True)
+
+    arrived = got[:, 8:10].reshape(LIVE, LANE)
+    finish = [lax.dynamic_slice(got, (d, 0, 0), (1, 16, LANE))[0] for d in owners]
+    arrived, finish = lax.optimization_barrier((arrived, finish))
+    correction = lax.all_gather(arrived[:MAX_LIVE], "col", axis=0, tiled=False).astype(F32)
     loads = panel_loads.reshape(cols, MB, LANE)
-    top = (loads[:, :LIVE].astype(F32) - live[None] * correction).astype(BF16)
-    loaded = jnp.concatenate([top, loads[:, LIVE:]], axis=1).reshape(cols * MB, LANE)
+    top = loads[:, :MAX_LIVE].astype(F32) - live[None, :MAX_LIVE] * correction
+    loaded = jnp.concatenate([top.astype(BF16), loads[:, MAX_LIVE:]], axis=1)
+    loaded = loaded.reshape(cols * MB, LANE)
     second_rows = jnp.dot(inverse_rows, loaded, preferred_element_type=F32).astype(BF16)
 
     pieces = [second_rows]
-    quads = []
     for p in range(NPAN):
-        owner = panel_block[p] // cols
-        piece = lax.dynamic_slice(got, (owner, 0, 0), (1, 24, LANE))[0]
-        pieces.append(piece[:16])
-        quads.append(piece[18:19])
-    pieces += quads + [jnp.zeros((14, LANE), BF16)]
+        pieces += [early[p][:8], finish[p][:8]]
+    pieces.append(jnp.concatenate([early[0][10:11, :48], early[1][10:11, :48], jnp.zeros((1, 32), BF16)], axis=1))
+    pieces.append(jnp.zeros((15, LANE), BF16))
     gathered = lax.all_gather(jnp.concatenate(pieces, axis=0), "col", axis=0, tiled=False)
     second = gathered[:, :MB].reshape(cols * MB, LANE)
     traces = jnp.dot(trace_map[0], second, preferred_element_type=F32).astype(BF16)
 
-    picked = []
-    for p in range(NPAN):
-        lane = panel_block[p] % cols
-        picked.append(lax.dynamic_slice(gathered, (lane, MB, 0), (1, 48, LANE))[0])
-    shared = jnp.concatenate([picked[0][:16], picked[1][16:32]], axis=0)
-    tail = jnp.concatenate([picked[0][32:33], picked[1][33:34], jnp.zeros((5, LANE), BF16)], axis=0)
+    core = lax.axis_index("col") % 2
+    own_lane = jnp.where(core == 0, lanes[0], lanes[1])
+    shared = lax.dynamic_slice(gathered, (own_lane, MB + 16 * core, 0), (1, 16, LANE))[0]
+    tails = [lax.dynamic_slice(gathered, (c, MB + 32, 0), (1, 1, LANE))[0] for c in lanes]
+    tail = jnp.where(jnp.arange(LANE, dtype=jnp.int32)[None, :] < 48, tails[0], tails[1])
+    last = jnp.stack([traces, jnp.broadcast_to(tail, (doms, LANE))], axis=1)
     sent = jnp.concatenate(
-        [
-            jnp.broadcast_to(shared[None], (doms, 32, LANE)),
-            traces[:, None],
-            jnp.broadcast_to(tail[None], (doms, 7, LANE)),
-        ],
-        axis=1,
+        [jnp.broadcast_to(shared.reshape(1, 8, 2, LANE), (doms, 8, 2, LANE)), last[:, None]], axis=1
     )
     got = lax.all_to_all(sent, "dom", 0, 0, tiled=True)
 
+    tiles = got[:, :8].reshape(doms, 16, LANE)
+    pairs = [(c, c ^ 1) for c in range(cols)]
+    other = lax.ppermute(tiles, "col", pairs)
     row_slots = surface_rows[0, 0].reshape(-1)
     landing = (jnp.arange(factor.shape[0], dtype=jnp.int32)[:, None] == row_slots[None, :]).astype(BF16)
-    surface_sum = jnp.dot(landing, got[:, 32], preferred_element_type=F32)
-    panels = []
-    quads = []
-    for p in range(NPAN):
-        block = got[:, 16 * p : 16 * p + 16].reshape(4, 16, 16, LANE)
-        panels.append(block.transpose(0, 2, 1, 3).reshape(P_SIZE, 16 * LANE))
-        quads.append(join3(got[:, 33 + p, :48]))
-    panel_factor = jnp.concatenate(panels, axis=0)
-    quads = jnp.concatenate(quads, axis=0).T
+    surface_sum = jnp.dot(landing, got[:, 8, 0], preferred_element_type=F32)
+    tail = got[:, 8, 1, :96].reshape(doms, NPAN, 48).transpose(1, 0, 2).reshape(NPAN * doms, 48)
+    quads = join3(tail).T
     panel_points = quads[:12].reshape(3, 4, NPAN * P_SIZE)
     panel_weights = quads[12:]
     shifted = colloc[:, :, None, None] - panel_points[:, None, :, :]
@@ -149,8 +147,19 @@
         4.0 * math.pi * jnp.sqrt(squared + SMOOTHING * SMOOTHING)
     )
     kernel_block = jnp.sum(panel_weights[None, :, :] * green_values, axis=1)
-    prior_update = lax.dot_general(
-        factor_low, panel_factor, (((1,), (1,)), ((), ())), preferred_element_type=F32
+
+    def prior(block):
+        panel = block.reshape(4, 16, 16, LANE).transpose(0, 2, 1, 3).reshape(P_SIZE, 16 * LANE)
+        return lax.dot_general(
+            factor_low, panel, (((1,), (1,)), ((), ())), preferred_element_type=F32
+        )
+
+    own_part = prior(tiles)
+    other_part = prior(other)
+    prior_update = jnp.where(
+        core == 0,
+        jnp.concatenate([own_part, other_part], axis=1),
+        jnp.concatenate([other_part, own_part], axis=1),
     )
     return kernel_block - surface_sum - prior_update
 

time: 115 us -> 116 us (level)
  blocking collectives: 39 us -> 55 us
  waiting for transfers between devices: 24 us -> 14.7 us
  starting transfers between devices: 30.6 us -> 24.1 us
    all_gather x0 -> x1, blocking collectives: none -> 22.4 us  [local(): lax.all_gather(arrived[:MAX_LIVE], 'col', axis=0, tiled=False).astype(F32)]
    all_to_all x1 -> x0, starting transfers between devices: 17.6 us -> none  [local(): arrived = lax.all_to_all(sent, ('dom', 'col'), 0, 0, tiled=True)]
    all_to_all x1 -> x0, waiting for transfers between devices: 10.9 us -> none  [local(): arrived = lax.all_to_all(sent, ('dom', 'col'), 0, 0, tiled=True)]
    all_to_all x1 -> x2, starting transfers between devices: 12.9 us -> 20.1 us  [local(): got = lax.all_to_all(sent, 'dom', 0, 0, tiled=True)]
    all_to_all x1, blocking collectives: 22.8 us -> 17.2 us  [local(): got = lax.all_to_all(sent, 'dom', 0, 0, tiled=True)]
    ppermute x0 -> x1, starting transfers between devices: none -> 3.99 us  [local(): other = lax.ppermute(tiles, 'col', pairs)]
    all_to_all x1 -> x2, waiting for transfers between devices: 13.1 us -> 14.5 us  [local(): got = lax.all_to_all(sent, 'dom', 0, 0, tiled=True)]
  transfers between devices with their start and end apart: 2 -> 3, of which waited for: 2 -> 3; matrix products, arithmetic and copies ran while one was open for 1% -> 1% of each run, Pallas kernels for 0% -> 0%
where the time goes in v2:
time: 116 us
  blocking collectives  55 us (47%)
  starting transfers between devices  24.1 us (21%)
  waiting for transfers between devices  14.7 us (13%)
  local copies, waits for them, and re-layouts  8.28 us (7%)
  between operations  5.7 us (5%)
  other arithmetic  5.31 us (5%)
  matrix products  2.63 us (2%)
    all_gather x1, blocking collectives, local(): lax.all_gather(arrived[:MAX_LIVE], 'col', axis=0, tiled=False).astype(F32)  22.4 us
    all_to_all x2, starting transfers between devices, local(): got = lax.all_to_all(sent, 'dom', 0, 0, tiled=True)  20.1 us
    all_to_all x1, blocking collectives, local(): got = lax.all_to_all(sent, 'dom', 0, 0, tiled=True)  17.2 us
    all_gather x1, blocking collectives, local(): lax.all_gather(jnp.concatenate(pieces, axis=0), 'col', axis=0, tiled=False)  15.3 us
    all_to_all x2, waiting for transfers between devices, local(): got = lax.all_to_all(sent, 'dom', 0, 0, tiled=True)  14.5 us
    ppermute x1, starting transfers between devices, local(): other = lax.ppermute(tiles, 'col', pairs)  3.99 us
    unnamed x19, local copies, waits for them, and re-layouts  2.57 us
  transfers between devices with their start and end apart: 3, of which 3 were waited for; matrix products, arithmetic and copies ran while one was open for 1% of the time, Pallas kernels for 0%

profile of v2, /device:TPU:1, one launch (start us, length us, event | category | flops | bytes accessed | tf_op | source)
XLA Modules:
  0.0 115.6 jit_solution(15966314834391583029)
XLA Ops:
  0.0 1.3 %dynamic_slice.24 = s32[1]{0:T(128)} dynamic-slice(s32[64]{0:T(128)} %param.17, s32[]{:T(128)S(6)} %select_n.102), dynamic_slice_sizes={1} | dynamic-slice | bytes 12 | tf_op jit(solution)/shard_map/dynamic_slice | solution.py:58
  1.3 0.6 compare_convert_fusion
  2.0 0.7 convert_bitcast_fusion.1
  2.6 0.7 copy.121
  3.3 0.7 reshape.85
  4.0 0.7 fusion.62
  4.7 0.1 copy.75
  4.8 0.1 copy.74
  4.9 0.1 copy.73
  5.0 0.1 copy.71
  5.3 0.1 copy.78
  5.4 0.1 copy.77
  5.5 0.1 copy.76
  5.6 0.1 concatenate.32
  6.1 0.9 copy-done.2
  7.0 0.1 copy-done.3
  7.1 0.3 fusion.1
  7.4 0.9 maximum_maximum_fusion
  8.2 13.1 %all-to-all-start = ((bf16[64,16,128]{2,1,0:T(8,128)(2,1)}), bf16[64,16,128]{2,1,0:T(8,128)(2,1)S(1)}, u32[]{:S(2)}, u32[]{:S(2)}) async-start(bf16[64,16,128]{2,1,0:T(8,128)(2,1)} %maximum_maximum_fusion), calls=%async_computation | async-start | bytes 524288 | tf_op jit(solution)/shard_map/all_to_all | solution.py:75
  21.3 0.6 fusion.73
  27.1 4.7 %all-to-all-done = bf16[64,16,128]{2,1,0:T(8,128)(2,1)S(1)} async-done(((bf16[64,16,128]{2,1,0:T(8,128)(2,1)}), bf16[64,16,128]{2,1,0:T(8,128)(2,1)S(1)}, u32[]{:S(2)}, u32[]{:S(2)}) %all-to-all-start) | async-done | bytes 262176 | tf_op jit(solution)/shard_map/all_to_all | solution.py:75
  32.2 0.6 slice_reduce_fusion.16
  32.8 0.3 fusion.3
  33.1 0.3 fusion.4
  33.5 0.8 maximum_maximum_fusion.1
  34.3 7.0 %all-to-all-start.1 = ((bf16[64,16,128]{2,1,0:T(8,128)(2,1)}), bf16[64,16,128]{2,1,0:T(8,128)(2,1)S(1)}, u32[]{:S(2)}, u32[]{:S(2)}) async-start(bf16[64,16,128]{2,1,0:T(8,128)(2,1)} %maximum_maximum_fusion.1), calls=%async_computation.1 | async-start | bytes 524288 | tf_op jit(solution)/shard_map/all_to_all | solution.py:102
  41.6 9.7 %all-to-all-done.1 = bf16[64,16,128]{2,1,0:T(8,128)(2,1)S(1)} async-done(((bf16[64,16,128]{2,1,0:T(8,128)(2,1)}), bf16[64,16,128]{2,1,0:T(8,128)(2,1)S(1)}, u32[]{:S(2)}, u32[]{:S(2)}) %all-to-all-start.1) | async-done | bytes 262176 | tf_op jit(solution)/shard_map/all_to_all | solution.py:102
  51.3 22.4 %all-gather = bf16[896,128]{1,0:T(8,128)(2,1)S(1)} all-gather(bf16[112,128]{1,0:T(8,128)(2,1)S(1)} %slice.204), channel_id=2, replica_groups=mesh['dom'=64,'col'=8] {'col'}, dimensions={0}, use_global_device_ids=true | all-gather | bytes 258048 | tf_op jit(solution)/shard_map/all_gather | solution.py:107
  73.7 0.1 fusion.8
  73.9 0.4 fusion
  74.3 0.2 concatenate.37
  74.5 15.3 %all-gather.1 = bf16[2048,128]{1,0:T(8,128)(2,1)S(1)} all-gather(bf16[256,128]{1,0:T(8,128)(2,1)S(1)} %concatenate.37), channel_id=3, replica_groups=mesh['dom'=64,'col'=8] {'col'}, dimensions={0}, use_global_device_ids=true | all-gather | bytes 589824 | tf_op jit(solution)/shard_map/all_gather | solution.py:119
  89.9 0.2 fusion.5
  90.2 0.1 broadcast_in_dim.178
  90.4 0.4 pad_maximum_fusion.1
  90.8 17.2 %all_to_all.15 = bf16[64,9,2,128]{3,2,1,0:T(2,128)(2,1)S(1)} all-to-all(bf16[64,9,2,128]{3,2,1,0:T(2,128)(2,1)S(1)} %pad_maximum_fusion.1), channel_id=1, replica_groups=mesh['dom'=64,'col'=8] {'dom'}, dimensions={0} | all-to-all | bytes 589824 | tf_op jit(solution)/shard_map/all_to_all | solution.py:132
  108.0 0.1 copy.94
  108.2 0.1 reshape.95
  108.3 0.2 slice.261
  108.6 0.2 copy.88
  108.8 4.0 %collective-permute-start = (bf16[64,16,128]{2,1,0:T(8,128)(2,1)S(1)}, bf16[64,16,128]{2,1,0:T(8,128)(2,1)S(1)}, u32[]{:S(2)}, u32[]{:S(2)}) collective-permute-start(bf16[64,16,128]{2,1,0:T(8,128)(2,1)S(1)} %copy.88), channel_id=1, source_target_pairs={{0,1},{1,0},{2,3},{3,2},{4,5},{5,4},{6,7},{7,6},{8,9},{9,8},{10,11... | collective-permute-start | bytes 786440 | tf_op jit(solution)/shard_map/ppermute | solution.py:136
  112.8 0.1 multiply_reduce_fusion
  112.9 0.5 multiply_reduce_fusion.1
  113.5 0.2 convolution_bitcast_fusion.1
  113.7 0.2 collective-permute-done
  114.0 0.2 convolution_bitcast_fusion
  114.2 0.6 copy-done.6
  114.9 0.7 fusion.2
  (66 shorter events, 1.5 us)
Async XLA Ops:
  0.0 89.9 %copy-start = (bf16[1,64,1664]{2,1,0:T(8,128)(2,1)S(1)}, bf16[1,64,1664]{2,1,0:T(8,128)(2,1)}, u32[]{:S(2)}) copy-start(bf16[1,64,1664]{2,1,0:T(8,128)(2,1)} %param.13) | copy-start | bytes 638980
  0.0 5.8 %copy-start.1 = (f32[64,2048]{1,0:T(8,128)S(1)}, f32[64,2048]{1,0:T(8,128)}, u32[]{:S(2)}) copy-start(f32[64,2048]{1,0:T(8,128)} %param.19) | copy-start | bytes 1572868
  5.9 1.1 copy-start.2
  5.9 1.2 %copy-start.3 = (bf16[1,1664,128]{2,1,0:T(8,128)(2,1)S(1)}, bf16[1,1664,128]{2,1,0:T(8,128)(2,1)}, u32[]{:S(2)}) copy-start(bf16[1,1664,128]{2,1,0:T(8,128)(2,1)} %param.14) | copy-start | bytes 1277956
  8.2 13.1 %copy-start.5 = (s32[2]{0:T(128)S(1)}, s32[2]{0:T(128)}, u32[]{:S(2)}) copy-start(s32[2]{0:T(128)} %param.23) | copy-start | bytes 28
  8.2 23.6 %all-to-all-start = ((bf16[64,16,128]{2,1,0:T(8,128)(2,1)}), bf16[64,16,128]{2,1,0:T(8,128)(2,1)S(1)}, u32[]{:S(2)}, u32[]{:S(2)}) async-start(bf16[64,16,128]{2,1,0:T(8,128)(2,1)} %maximum_maximum_fusion), calls=%async_computation | async-start | bytes 524288 | tf_op jit(solution)/shard_map/all_to_all | solution.py:75
  34.3 17.0 %all-to-all-start.1 = ((bf16[64,16,128]{2,1,0:T(8,128)(2,1)}), bf16[64,16,128]{2,1,0:T(8,128)(2,1)S(1)}, u32[]{:S(2)}, u32[]{:S(2)}) async-start(bf16[64,16,128]{2,1,0:T(8,128)(2,1)} %maximum_maximum_fusion.1), calls=%async_computation.1 | async-start | bytes 524288 | tf_op jit(solution)/shard_map/all_to_all | solution.py:102
  108.6 4.2 %copy-start.4 = (f32[3,64]{1,0:T(4,128)S(1)}, f32[3,64]{1,0:T(4,128)}, u32[]{:S(2)}) copy-start(f32[3,64]{1,0:T(4,128)} %param.20) | copy-start | bytes 2308
  108.8 5.1 %collective-permute-start = (bf16[64,16,128]{2,1,0:T(8,128)(2,1)S(1)}, bf16[64,16,128]{2,1,0:T(8,128)(2,1)S(1)}, u32[]{:S(2)}, u32[]{:S(2)}) collective-permute-start(bf16[64,16,128]{2,1,0:T(8,128)(2,1)S(1)} %copy.88), channel_id=1, source_target_pairs={{0,1},{1,0},{2,3},{3,2},{4,5},{5,4},{6,7},{7,6},{8,9},{9,8},{10,11... | collective-permute-start | bytes 786440 | tf_op jit(solution)/shard_map/ppermute | solution.py:136
  114.2 0.7 copy-start.6

commit v3 on v2

v3 whole, which is shorter than its diff:
```python
import math

import jax
import jax.numpy as jnp
from jax import lax
from jax.experimental import pallas as pl
from jax.experimental.pallas import tpu as pltpu
from jax.sharding import PartitionSpec as P

MB = 208
P_SIZE = 64
NPAN = 2
LIVE = 128
MAX_LIVE = 112
LANE = 128

WAVE_NUMBER = 8.0
SMOOTHING = 0.05

F32 = jnp.float32
BF16 = jnp.bfloat16
VM = pl.BlockSpec(memory_space=pltpu.VMEM)
SM = pl.BlockSpec(memory_space=pltpu.SMEM)
PARAMS = pltpu.CompilerParams(vmem_limit_bytes=16 * 1024 * 1024)


def iota(shape, axis):
    return lax.broadcasted_iota(jnp.int32, shape, axis)


def terms(values):
    high = values.astype(BF16).astype(F32)
    rest = values - high
    middle = rest.astype(BF16).astype(F32)
    return high, middle, rest - middle


def turned(left, right):
    return lax.dot_general(
        left, right.astype(BF16), (((1,), (1,)), ((), ())), preferred_element_type=F32
    )


def first_kernel(
    inv_hbm, map_hbm, loads_hbm, coup_hbm, listed_hbm, count_hbm, rows_hbm, factor_hbm, colloc_hbm,
    points_hbm, weight_hbm,
    sent_ref, late_ref, inv_ref, map_ref, loads_ref, low_ref, landing_ref, spots_ref,
    coup_in, listed_ref, count_ref, rows_ref, factor_ref, colloc_ref, points_ref, weight_ref,
    quad_ref, coup_scr, spot_scr, first_ref, row_ref, sems,
):
    doms = sent_ref.shape[0]
    moves = [
        pltpu.make_async_copy(src, dst, sems.at[i])
        for i, (src, dst) in enumerate(
            [
                (listed_hbm, listed_ref),
                (count_hbm, count_ref),
                (points_hbm, points_ref),
                (weight_hbm, weight_ref),
                (coup_hbm, coup_in),
                (rows_hbm, rows_ref),
                (colloc_hbm, colloc_ref),
                (factor_hbm, factor_ref),
                (loads_hbm, loads_ref),
                (inv_hbm, inv_ref),
                (map_hbm, map_ref),
            ]
        )
    ]
    for move in moves:
        move.start()
    coup_scr[...] = jnp.zeros_like(coup_scr)
    row_ref[...] = jnp.zeros_like(row_ref)
    spot_scr[...] = jnp.zeros_like(spot_scr)
    for move in moves[:7]:
        move.wait()
    count = count_ref[lax.axis_index("dom")]
    for c in range(3):
        quad_ref[4 * c : 4 * c + 4, :] = points_ref[c]
    quad_ref[12:16, :] = weight_ref[...]
    for k in range(6):
        coup_scr[k : k + 1, :] = coup_in[k][:, :LIVE]
    spot_scr[0:3, :] = colloc_ref[...]
    quads = jnp.concatenate(list(terms(quad_ref[...])) + [jnp.zeros((80, doms), F32)], axis=0)
    weights = list(terms(coup_scr[...]))
    even = jnp.concatenate([jnp.zeros((48, LIVE), F32)] + weights + [jnp.zeros((56, LIVE), F32)], axis=0)
    odd = jnp.concatenate([jnp.zeros((72, LIVE), F32)] + weights + [jnp.zeros((32, LIVE), F32)], axis=0)
    spots = jnp.concatenate(list(terms(spot_scr[...])) + [jnp.zeros((104, doms), F32)], axis=0)
    at = iota((doms, LIVE), 1)
    pair = 2 * iota((doms, LIVE), 0)
    unit = (iota((doms, doms), 0) == iota((doms, doms), 1)).astype(BF16)
    misc = turned(unit, quads)
    misc = misc + turned((at == pair).astype(BF16), even)
    misc = misc + turned((at == pair + 1).astype(BF16), odd)
    for k in range(6):
        misc = jnp.where(at == 96 + k, listed_ref[0, k].astype(F32), misc)
    misc = jnp.where(at == 102, count.astype(F32), misc)
    row_ref[pl.ds(2, doms, stride=8), :] = misc
    spots_ref[...] = turned(unit, spots)
    landing_ref[...] = (iota((doms, doms), 0) == rows_ref[0, 0]).astype(BF16)
    moves[7].wait()
    for h in range(doms):
        rows = pl.ds(8 * (h // 16), 8)
        lanes = pl.ds(LANE * (h % 16), LANE)
        sent_ref[h, :8, :] = factor_ref[rows, lanes].astype(BF16)
        rows = pl.ds(8 * (h // 16) + 32, 8)
        late_ref[h] = factor_ref[rows, lanes].astype(BF16)
    low_ref[...] = factor_ref[...].astype(BF16)
    for move in moves[8:10]:
        move.wait()
    first = jnp.dot(inv_ref[0, :LIVE, :], loads_ref[0], preferred_element_type=F32)
    first_ref[...] = jnp.where(iota((LIVE, LANE), 0) < count, first, 0.0)
    row_ref[pl.ds(0, doms, stride=8), :] = first_ref[pl.ds(0, doms, stride=2), :]
    row_ref[pl.ds(1, doms, stride=8), :] = first_ref[pl.ds(1, doms, stride=2), :]
    for h in range(doms):
        sent_ref[h, 8:16, :] = row_ref[8 * h : 8 * h + 8, :].astype(BF16)
    moves[10].wait()


def first_stage(
    inverse, trace_map, panel_coupling, coupling, neighbours, iface_count, surface_rows, factor,
    colloc, quad_points, quad_weight, doms,
):
    shape = jax.ShapeDtypeStruct
    coupling = coupling.transpose(1, 0, 2)
    return pl.pallas_call(
        first_kernel,
        out_shape=(
            shape((doms, 16, LANE), BF16),
            shape((doms, 8, LANE), BF16),
            shape(inverse.shape, BF16),
            shape(trace_map.shape, BF16),
            shape(panel_coupling.shape, BF16),
            shape(factor.shape, BF16),
            shape((doms, doms), BF16),
            shape((doms, LANE), F32),
        ),
        in_specs=[pl.BlockSpec(memory_space=pltpu.HBM)] * 11,
        out_specs=(VM,) * 8,
        scratch_shapes=[
            pltpu.VMEM(coupling.shape, F32),
            pltpu.SMEM(neighbours.shape, jnp.int32),
            pltpu.SMEM(iface_count.shape, jnp.int32),
            pltpu.VMEM(surface_rows.shape, jnp.int32),
            pltpu.VMEM(factor.shape, F32),
            pltpu.VMEM(colloc.shape, F32),
            pltpu.VMEM(quad_points.shape, F32),
            pltpu.VMEM(quad_weight.shape, F32),
            pltpu.VMEM((16, doms), F32),
            pltpu.VMEM((8, LIVE), F32),
            pltpu.VMEM((8, doms), F32),
            pltpu.VMEM((LIVE, LANE), F32),
            pltpu.VMEM((8 * doms, LANE), F32),
            pltpu.SemaphoreType.DMA((11,)),
        ],
        compiler_params=PARAMS,
        name="first_stage",
    )(
        *(
            pltpu.with_memory_space_constraint(x, pltpu.HBM)
            for x in (
                inverse, trace_map, panel_coupling, coupling, neighbours, iface_count, surface_rows,
                factor, colloc, quad_points, quad_weight,
            )
        )
    )


def mix_kernel(got_ref, late_ref, block_ref, sent_ref, early_ref, quad_ref, row_ref):
    doms = got_ref.shape[0]
    cols = lax.axis_size("col")
    for h in range(doms):
        row_ref[8 * h : 8 * h + 8, :] = got_ref[h, 8:16, :].astype(F32)
    misc = row_ref[pl.ds(2, doms, stride=8), :]
    weights = misc + pltpu.roll(misc, LANE - 8, 1) + pltpu.roll(misc, LANE - 16, 1)
    sources = iota((doms, doms), 1).astype(F32)
    mixed = []
    for r in range(2):
        mixing = jnp.zeros((doms, doms), F32)
        for k in range(6):
            lane = 48 + 24 * r + k
            mixing = mixing + jnp.where(
                misc[:, 96 + k : 97 + k] == sources, weights[:, lane : lane + 1], 0.0
            )
        summed = jnp.dot(
            mixing,
            row_ref[pl.ds(r, doms, stride=8), :],
            precision=lax.Precision.HIGHEST,
            preferred_element_type=F32,
        )
        row = (2 * lax.axis_index("dom") + r).astype(F32)
        mixed.append(jnp.where(misc[:, 102:103] > row, summed, 0.0))
    for p in range(NPAN):
        owner = block_ref[p] // cols
        early_ref[p] = got_ref[pl.ds(owner, 1)][0, :8, :]
        quad_ref[p] = got_ref[pl.ds(owner, 1)][0, 8:16, :]
    row_ref[pl.ds(0, doms, stride=8), :] = mixed[0]
    row_ref[pl.ds(1, doms, stride=8), :] = mixed[1]
    for h in range(doms):
        sent_ref[h, :8, :] = late_ref[h]
        sent_ref[h, 8:16, :] = row_ref[8 * h : 8 * h + 8, :].astype(BF16)


def mix_stage(got, late, panel_block):
    doms = got.shape[0]
    return pl.pallas_call(
        mix_kernel,
        out_shape=(
            jax.ShapeDtypeStruct((doms, 16, LANE), BF16),
            jax.ShapeDtypeStruct((NPAN, 8, LANE), BF16),
            jax.ShapeDtypeStruct((NPAN, 8, LANE), BF16),
        ),
        in_specs=[VM, VM, SM],
        out_specs=(VM, VM, VM),
        scratch_shapes=[pltpu.VMEM((8 * doms, LANE), F32)],
        compiler_params=PARAMS,
        name="mix_stage",
    )(got, late, panel_block)


def second_kernel(
    correction_ref, loads_ref, inv_ref, got_ref, early_ref, quad_ref, block_ref, out_ref, loaded_ref
):
    cols = correction_ref.shape[0]
    for c in range(cols):
        top = loads_ref[0, MB * c : MB * c + MAX_LIVE, :].astype(F32) - correction_ref[c].astype(F32)
        loaded_ref[MB * c : MB * c + MAX_LIVE, :] = top.astype(BF16)
        loaded_ref[MB * c + MAX_LIVE : MB * (c + 1), :] = loads_ref[0, MB * c + MAX_LIVE : MB * (c + 1), :]
    second = jnp.dot(inv_ref[0], loaded_ref[...], preferred_element_type=F32)
    out_ref[:MB, :] = second.astype(BF16)
    for p in range(NPAN):
        owner = lax.div(block_ref[p], cols)
        out_ref[MB + 16 * p : MB + 16 * p + 8, :] = early_ref[p]
        out_ref[MB + 16 * p + 8 : MB + 16 * p + 16, :] = got_ref[pl.ds(owner, 1)][0, :8, :]
        out_ref[MB + 32 + 8 * p : MB + 40 + 8 * p, :] = quad_ref[p]


def second_stage(correction, loads, inverse, got, early, quads, panel_block):
    return pl.pallas_call(
        second_kernel,
        out_shape=jax.ShapeDtypeStruct((MB + 48, LANE), BF16),
        in_specs=[VM] * 6 + [SM],
        out_specs=VM,
        scratch_shapes=[pltpu.VMEM(loads.shape[1:], BF16)],
        compiler_params=PARAMS,
        name="second_stage",
    )(correction, loads, inverse, got, early, quads, panel_block)


def trace_kernel(gathered_ref, map_ref, block_ref, shared_ref, last_ref, second_ref, row_ref):
    cols = gathered_ref.shape[0]
    doms = map_ref.shape[1]
    core = lax.rem(lax.axis_index("col"), 2)
    for c in range(cols):
        second_ref[MB * c : MB * (c + 1), :] = gathered_ref[c, :MB, :]
    traces = jnp.dot(map_ref[0], second_ref[...], preferred_element_type=F32)
    lanes = [lax.rem(block_ref[p], cols) for p in range(NPAN)]
    own = jnp.where(core == 0, lanes[0], lanes[1])
    first = gathered_ref[pl.ds(own, 1)][0, MB : MB + 16, :]
    second = gathered_ref[pl.ds(own, 1)][0, MB + 16 : MB + 32, :]
    shared_ref[...] = jnp.where(core == 0, first.astype(F32), second.astype(F32)).astype(BF16)
    quads = [
        gathered_ref[pl.ds(lanes[p], 1)][0, MB + 32 : MB + 48, :].astype(F32)[8 * p + 2 : 8 * p + 3, :]
        for p in range(NPAN)
    ]
    tail = jnp.where(iota((1, LANE), 1) < 48, quads[0], pltpu.roll(quads[1], 48, 1))
    row_ref[pl.ds(0, doms, stride=2), :] = traces
    row_ref[pl.ds(1, doms, stride=2), :] = jnp.broadcast_to(tail, (doms, LANE))
    last_ref[...] = row_ref[...].astype(BF16)


def trace_stage(gathered, trace_map, panel_block):
    doms = trace_map.shape[1]
    return pl.pallas_call(
        trace_kernel,
        out_shape=(
            jax.ShapeDtypeStruct((16, LANE), BF16),
            jax.ShapeDtypeStruct((2 * doms, LANE), BF16),
        ),
        in_specs=[VM, VM, SM],
        out_specs=(VM, VM),
        scratch_shapes=[
            pltpu.VMEM((trace_map.shape[2], LANE), BF16),
            pltpu.VMEM((2 * doms, LANE), F32),
        ],
        compiler_params=PARAMS,
        name="trace_stage",
    )(gathered, trace_map, panel_block)


def join3(parts):
    parts = parts.astype(F32)
    width = parts.shape[-1] // 3
    return (parts[..., 2 * width :] + parts[..., width : 2 * width]) + parts[..., :width]


def local(
    inverse,
    trace_map,
    panel_coupling,
    coupling,
    neighbours,
    iface_count,
    surface_rows,
    factor,
    colloc,
    quad_points,
    quad_weight,
    panel_block,
):
    doms = lax.axis_size("dom")
    cols = lax.axis_size("col")
    sent, late, inverse, trace_map, loads, factor_low, landing, spots = first_stage(
        inverse, trace_map, panel_coupling, coupling, neighbours, iface_count, surface_rows, factor,
        colloc, quad_points, quad_weight, doms,
    )
    got = lax.all_to_all(sent, "dom", 0, 0, tiled=True)
    sent, early, quads = mix_stage(got, late, panel_block)
    got = lax.all_to_all(sent, "dom", 0, 0, tiled=True)

    arrived = got[:, 8:10].reshape(LIVE, LANE)
    correction = lax.all_gather(arrived[:MAX_LIVE], "col", axis=0, tiled=False)
    pieces = second_stage(correction, loads, inverse, got, early, quads, panel_block)
    gathered = lax.all_gather(pieces, "col", axis=0, tiled=False)
    shared, last = trace_stage(gathered, trace_map, panel_block)

    core = lax.axis_index("col") % 2
    sent = jnp.concatenate(
        [
            jnp.broadcast_to(shared.reshape(1, 8, 2, LANE), (doms, 8, 2, LANE)),
            last.reshape(doms, 1, 2, LANE),
        ],
        axis=1,
    )
    got = lax.all_to_all(sent, "dom", 0, 0, tiled=True)

    tiles = got[:, :8].reshape(doms, 16, LANE)
    pairs = [(c, c ^ 1) for c in range(cols)]
    other = lax.ppermute(tiles, "col", pairs)
    surface_sum = jnp.dot(landing, got[:, 8, 0], preferred_element_type=F32)
    tail = got[:, 8, 1, :96].reshape(doms, NPAN, 48).transpose(1, 0, 2).reshape(NPAN * doms, 48)
    quads = join3(tail).T
    panel_points = quads[:12].reshape(3, 4, NPAN * P_SIZE)
    panel_weights = quads[12:]
    spots = (spots[:, 16:19] + spots[:, 8:11]) + spots[:, 0:3]
    shifted = spots.T[:, :, None, None] - panel_points[:, None, :, :]
    squared = jnp.sum(shifted * shifted, axis=0)
    green_values = jnp.cos(WAVE_NUMBER * jnp.sqrt(squared)) / (
        4.0 * math.pi * jnp.sqrt(squared + SMOOTHING * SMOOTHING)
    )
    kernel_block = jnp.sum(panel_weights[None, :, :] * green_values, axis=1)

    def prior(block):
        panel = block.reshape(4, 16, 2, 8, LANE).transpose(2, 0, 3, 1, 4).reshape(P_SIZE, 16 * LANE)
        return lax.dot_general(
            factor_low, panel, (((1,), (1,)), ((), ())), preferred_element_type=F32
        )

    own_part = prior(tiles)
    other_part = prior(other)
    prior_update = jnp.where(
        core == 0,
        jnp.concatenate([own_part, other_part], axis=1),
        jnp.concatenate([other_part, own_part], axis=1),
    )
    return kernel_block - surface_sum - prior_update


def solution(mesh):
    in_specs = (
        P("dom", "col", None),
        P("dom", "col", None),
        P("dom", None, None),
        P("dom", None, "col"),
        P("dom", None),
        P(),
        P("dom", "col", None, None),
        P(("dom", "col"), None),
        P(None, ("dom", "col")),
        P(None, None, ("dom", "col")),
        P(None, ("dom", "col")),
        P(),
    )
    out_specs = P(("dom", "col"), None)
    return jax.shard_map(local, mesh=mesh, in_specs=in_specs, out_specs=out_specs, check_vma=False)
```

time: 116 us -> 109 us (0.940)
  blocking collectives: 55 us -> 77.8 us
  starting transfers between devices: 24.1 us -> 9.76 us
  local copies, waits for them, and re-layouts: 8.28 us -> 1.71 us
  between operations: 5.7 us -> 0.17 us
  Pallas kernels: 0 us -> 4.71 us
  other arithmetic: 5.31 us -> 1.83 us
  waiting for transfers between devices: 14.7 us -> 11.5 us
  matrix products: 2.63 us -> 1.18 us
    all_to_all x1 -> x2, blocking collectives: 17.2 us -> 40 us  [local(): got = lax.all_to_all(sent, 'dom', 0, 0, tiled=True)]
    all_to_all x2 -> x1, starting transfers between devices: 20.1 us -> 5.77 us  [local(): got = lax.all_to_all(sent, 'dom', 0, 0, tiled=True)]
    pallas_call x0 -> x4, Pallas kernels: none -> 4.71 us  [the longest x1 1.9 us: first_stage(): pl.pallas_call(first_kernel, out_shape=(shape((doms, 16, LANE), BF16), sh...]
    all_to_all x2 -> x1, waiting for transfers between devices: 14.5 us -> 11.5 us  [local(): got = lax.all_to_all(sent, 'dom', 0, 0, tiled=True)]
    concatenate x4 -> x0, other arithmetic: 1.81 us -> none  [the longest x1 0.86 us: local(): jnp.concatenate([chunks[:, :8], first_values, misc[:, None], jnp.zeros((d...]
    unnamed x19 -> x4, local copies, waits for them, and re-layouts: 2.57 us -> 0.83 us
    convert_element_type x6 -> x0, other arithmetic: 1.58 us -> none  [the longest x2 0.7 us: split3(): low.astype(BF16)]
    slice x16 -> x1, local copies, waits for them, and re-layouts: 1.48 us -> 0.02 us  [local(): correction = lax.all_gather(arrived[:MAX_LIVE], 'col', axis=0, tiled=False)]
  transfers between devices with their start and end apart: 3 -> 2, of which waited for: 3 -> 1; matrix products, arithmetic and copies ran while one was open for 1% -> 1% of each run, Pallas kernels for 0% -> 0%
where the time goes in v3:
time: 109 us
  blocking collectives  77.8 us (71%)
  waiting for transfers between devices  11.5 us (11%)
  starting transfers between devices  9.76 us (9%)
  Pallas kernels  4.71 us (4%)
  other arithmetic  1.83 us (2%)
  local copies, waits for them, and re-layouts  1.71 us (2%)
  matrix products  1.18 us (1%)
    all_to_all x2, blocking collectives, local(): got = lax.all_to_all(sent, 'dom', 0, 0, tiled=True)  40 us
    all_gather x1, blocking collectives, local(): correction = lax.all_gather(arrived[:MAX_LIVE], 'col', axis=0, tiled=False)  22.4 us
    all_gather x1, blocking collectives, local(): gathered = lax.all_gather(pieces, 'col', axis=0, tiled=False)  15.3 us
    all_to_all x1, waiting for transfers between devices, local(): got = lax.all_to_all(sent, 'dom', 0, 0, tiled=True)  11.5 us
    all_to_all x1, starting transfers between devices, local(): got = lax.all_to_all(sent, 'dom', 0, 0, tiled=True)  5.77 us
    ppermute x1, starting transfers between devices, local(): other = lax.ppermute(tiles, 'col', pairs)  3.99 us
  transfers between devices with their start and end apart: 2, of which 1 were waited for; matrix products, arithmetic and copies ran while one was open for 1% of the time, Pallas kernels for 0%

profile of v3, /device:TPU:1, one launch (start us, length us, event | category | flops | bytes accessed | tf_op | source)
XLA Modules:
  0.0 108.6 jit_solution(16114683812638981026)
XLA Ops:
  0.0 1.9 %first_stage.1 = (bf16[64,16,128]{2,1,0:T(8,128)(2,1)S(1)}, bf16[64,8,128]{2,1,0:T(8,128)(2,1)S(1)}, bf16[1,208,1664]{2,1,0:T(8,128)(2,1)S(1)}, bf16[1,64,1664]{...) custom-call(bf16[1,208,1664]{2,1,0:T(8,128)(2,1)} %inv_hbm.1, ...), custom_call_target="tpu_custom_call" | custom-call | tf_op jit(solution)/shard_map/first_stage/pallas_call | solution.py:126
  1.9 23.2 %all_to_all.15.got_ref = bf16[64,16,128]{2,1,0:T(8,128)(2,1)S(1)} all-to-all(bf16[64,16,128]{2,1,0:T(8,128)(2,1)S(1)} %get-tuple-element.18), channel_id=1, replica_groups=mesh['dom'=64,'col'=8] {'dom'}, dimensions={0} | all-to-all | bytes 524288 | tf_op jit(solution)/shard_map/all_to_all | solution.py:317
  25.2 0.0 copy-start
  25.2 0.7 copy-done
  25.8 1.1 %mix_stage.1 = (bf16[64,16,128]{2,1,0:T(8,128)(2,1)S(1)}, bf16[2,8,128]{2,1,0:T(8,128)(2,1)S(1)}, bf16[2,8,128]{2,1,0:T(8,128)(2,1)S(1)}) custom-call(bf16[64,16,128]{2,1,0:T(8,128)(2,1)S(1)} %all_to_all.15.got_ref, bf16[64,8,128]{2,1,0:T(8,128)(2,1)S(1)} %get-tuple-element.19.late_ref, s32[2]{0:T(128)S(1)} %copy-done), custom_call_target="tpu_custom_call" | custom-call | tf_op jit(solution)/shard_map/mix_stage/pallas_call | solution.py:206
  26.9 16.8 %all_to_all.16.got_ref = bf16[64,16,128]{2,1,0:T(8,128)(2,1)S(1)} all-to-all(bf16[64,16,128]{2,1,0:T(8,128)(2,1)S(1)} %get-tuple-element.20), channel_id=1, replica_groups=mesh['dom'=64,'col'=8] {'dom'}, dimensions={0} | all-to-all | bytes 524288 | tf_op jit(solution)/shard_map/all_to_all | solution.py:319
  43.7 22.4 %all_gather.13.correction_ref = bf16[8,112,128]{2,1,0:T(8,128)(2,1)S(1)} all-gather(bf16[1,112,128]{2,1,0:T(8,128)(2,1)S(1)} %bitcast.49), channel_id=1, replica_groups=mesh['dom'=64,'col'=8] {'col'}, dimensions={0}, use_global_device_ids=true | all-gather | bytes 258048 | tf_op jit(solution)/shard_map/all_gather | solution.py:322
  66.1 0.9 second_stage.1
  67.1 15.3 %all-gather = bf16[2048,128]{1,0:T(8,128)(2,1)S(1)} all-gather(bf16[256,128]{1,0:T(8,128)(2,1)S(1)} %second_stage.1), channel_id=2, replica_groups=mesh['dom'=64,'col'=8] {'col'}, dimensions={0}, use_global_device_ids=true | all-gather | bytes 589824 | tf_op jit(solution)/shard_map/all_gather | solution.py:324
  82.4 0.8 trace_stage.1
  83.2 0.1 broadcast_in_dim.10
  83.3 1.1 %pad_maximum_fusion = bf16[64,9,2,128]{3,2,1,0:T(2,128)(2,1)} fusion(bf16[64,1,2,128]{3,2,1,0:T(2,128)(2,1)S(1)} %bitcast.42, bf16[64,8,2,128]{3,2,1,0:T(2,128)(2,1)S(1)} %broadcast_in_dim.10), kind=kLoop, calls=%fused_computation.3 | loop fusion | flops 147456 | bytes 589824 | tf_op jit(solution)/shard_map/concatenate | solution.py:328
  84.4 5.8 %all-to-all-start.2 = ((bf16[64,9,2,128]{3,2,1,0:T(2,128)(2,1)}), bf16[64,9,2,128]{3,2,1,0:T(2,128)(2,1)S(1)}, u32[]{:S(2)}, u32[]{:S(2)}) async-start(bf16[64,9,2,128]{3,2,1,0:T(2,128)(2,1)} %pad_maximum_fusion), calls=%async_computation.2 | async-start | bytes 589824 | tf_op jit(solution)/shard_map/all_to_all | solution.py:335
  90.2 0.1 add_bitcast_fusion
  90.3 0.1 copy.42
  90.4 11.5 %all-to-all-done.2 = bf16[64,9,2,128]{3,2,1,0:T(2,128)(2,1)S(1)} async-done(((bf16[64,9,2,128]{3,2,1,0:T(2,128)(2,1)}), bf16[64,9,2,128]{3,2,1,0:T(2,128)(2,1)S(1)}, u32[]{:S(2)}, u32[]{:S(2)}) %all-to-all-start.2) | async-done | bytes 294944 | tf_op jit(solution)/shard_map/all_to_all | solution.py:335
  101.9 0.2 slice.59
  102.0 0.1 copy.50
  102.1 0.2 copy.46
  102.3 4.0 %collective-permute-start = (bf16[64,16,128]{2,1,0:T(8,128)(2,1)S(1)}, bf16[64,16,128]{2,1,0:T(8,128)(2,1)S(1)}, u32[]{:S(2)}, u32[]{:S(2)}) collective-permute-start(bf16[64,16,128]{2,1,0:T(8,128)(2,1)S(1)} %copy.46), channel_id=1, source_target_pairs={{0,1},{1,0},{2,3},{3,2},{4,5},{5,4},{6,7},{7,6},{8,9},{9,8},{10,11... | collective-permute-start | bytes 786440 | tf_op jit(solution)/shard_map/ppermute | solution.py:339
  106.3 0.1 copy.48
  106.5 0.1 reshape.33
  106.6 0.1 multiply_reduce_fusion
  106.7 0.5 multiply_reduce_fusion.1
  107.3 0.2 fusion.4
  107.6 0.0 collective-permute-done
  107.6 0.1 copy.47
  107.6 0.2 fusion.1
  107.9 0.7 fusion
  (9 shorter events, 0.2 us)
Async XLA Ops:
  25.2 0.7 copy-start
  84.4 17.4 %all-to-all-start.2 = ((bf16[64,9,2,128]{3,2,1,0:T(2,128)(2,1)}), bf16[64,9,2,128]{3,2,1,0:T(2,128)(2,1)S(1)}, u32[]{:S(2)}, u32[]{:S(2)}) async-start(bf16[64,9,2,128]{3,2,1,0:T(2,128)(2,1)} %pad_maximum_fusion), calls=%async_computation.2 | async-start | bytes 589824 | tf_op jit(solution)/shard_map/all_to_all | solution.py:335
  102.3 5.3 %collective-permute-start = (bf16[64,16,128]{2,1,0:T(8,128)(2,1)S(1)}, bf16[64,16,128]{2,1,0:T(8,128)(2,1)S(1)}, u32[]{:S(2)}, u32[]{:S(2)}) collective-permute-start(bf16[64,16,128]{2,1,0:T(8,128)(2,1)S(1)} %copy.46), channel_id=1, source_target_pairs={{0,1},{1,0},{2,3},{3,2},{4,5},{5,4},{6,7},{7,6},{8,9},{9,8},{10,11... | collective-permute-start | bytes 786440 | tf_op jit(solution)/shard_map/ppermute | solution.py:339

commit v4 on v3

v4 whole, which is shorter than its diff:
```python
import math

import jax
import jax.numpy as jnp
from jax import lax
from jax.experimental import pallas as pl
from jax.experimental.pallas import tpu as pltpu
from jax.sharding import PartitionSpec as P

MB = 208
P_SIZE = 64
NPAN = 2
LIVE = 128
MAX_LIVE = 112
LANE = 128
ROWS = 20

WAVE_NUMBER = 8.0
SMOOTHING = 0.05

F32 = jnp.float32
BF16 = jnp.bfloat16
VM = pl.BlockSpec(memory_space=pltpu.VMEM)
PARAMS = pltpu.CompilerParams(vmem_limit_bytes=16 * 1024 * 1024)


def iota(shape, axis):
    return lax.broadcasted_iota(jnp.int32, shape, axis)


def terms(values):
    high = values.astype(BF16).astype(F32)
    rest = values - high
    middle = rest.astype(BF16).astype(F32)
    return high, middle, rest - middle


def turned(left, right):
    return lax.dot_general(
        left, right.astype(BF16), (((1,), (1,)), ((), ())), preferred_element_type=F32
    )


def first_kernel(
    inv_hbm, map_hbm, loads_hbm, coup_hbm, listed_hbm, count_hbm, rows_hbm, factor_hbm, colloc_hbm,
    points_hbm, weight_hbm,
    sent_ref, inv_ref, map_ref, loads_ref, low_ref, landing_ref, spots_ref,
    coup_in, listed_ref, count_ref, rows_ref, factor_ref, colloc_ref, points_ref, weight_ref,
    quad_ref, coup_scr, spot_scr, first_ref, row_ref, sems,
):
    doms = landing_ref.shape[1]
    moves = [
        pltpu.make_async_copy(src, dst, sems.at[i])
        for i, (src, dst) in enumerate(
            [
                (listed_hbm, listed_ref),
                (count_hbm, count_ref),
                (points_hbm, points_ref),
                (weight_hbm, weight_ref),
                (coup_hbm, coup_in),
                (rows_hbm, rows_ref),
                (colloc_hbm, colloc_ref),
                (factor_hbm, factor_ref),
                (loads_hbm, loads_ref),
                (inv_hbm, inv_ref),
                (map_hbm, map_ref),
            ]
        )
    ]
    for move in moves:
        move.start()
    coup_scr[...] = jnp.zeros_like(coup_scr)
    row_ref[...] = jnp.zeros_like(row_ref)
    spot_scr[...] = jnp.zeros_like(spot_scr)
    for move in moves[:7]:
        move.wait()
    count = count_ref[lax.axis_index("dom")]
    for c in range(3):
        quad_ref[4 * c : 4 * c + 4, :] = points_ref[c]
    quad_ref[12:16, :] = weight_ref[...]
    for k in range(6):
        coup_scr[k : k + 1, :] = coup_in[k][:, :LIVE]
    spot_scr[0:3, :] = colloc_ref[...]
    quads = jnp.concatenate(list(terms(quad_ref[...])) + [jnp.zeros((80, doms), F32)], axis=0)
    weights = list(terms(coup_scr[...]))
    even = jnp.concatenate([jnp.zeros((48, LIVE), F32)] + weights + [jnp.zeros((56, LIVE), F32)], axis=0)
    odd = jnp.concatenate([jnp.zeros((72, LIVE), F32)] + weights + [jnp.zeros((32, LIVE), F32)], axis=0)
    spots = jnp.concatenate(list(terms(spot_scr[...])) + [jnp.zeros((104, doms), F32)], axis=0)
    at = iota((doms, LIVE), 1)
    pair = 2 * iota((doms, LIVE), 0)
    unit = (iota((doms, doms), 0) == iota((doms, doms), 1)).astype(BF16)
    misc = turned(unit, quads)
    misc = misc + turned((at == pair).astype(BF16), even)
    misc = misc + turned((at == pair + 1).astype(BF16), odd)
    for k in range(6):
        misc = jnp.where(at == 96 + k, listed_ref[0, k].astype(F32), misc)
    misc = jnp.where(at == 102, count.astype(F32), misc)
    row_ref[pl.ds(2, doms, stride=4), :] = misc
    spots = turned(unit, spots)
    spots_ref[...] = spots + pltpu.roll(spots, LANE - 8, 1) + pltpu.roll(spots, LANE - 16, 1)
    landing_ref[...] = (iota((doms, doms), 0) == rows_ref[0, 0]).astype(BF16)
    moves[7].wait()
    for h in range(doms):
        tile = factor_ref[pl.ds(16 * (h // 16), 16), pl.ds(LANE * (h % 16), LANE)]
        sent_ref[ROWS * h : ROWS * h + 16, :] = tile.astype(BF16)
    low_ref[...] = factor_ref[...].astype(BF16)
    for move in moves[8:10]:
        move.wait()
    first = jnp.dot(inv_ref[0, :LIVE, :], loads_ref[0], preferred_element_type=F32)
    first_ref[...] = jnp.where(iota((LIVE, LANE), 0) < count, first, 0.0)
    row_ref[pl.ds(0, doms, stride=4), :] = first_ref[pl.ds(0, doms, stride=2), :]
    row_ref[pl.ds(1, doms, stride=4), :] = first_ref[pl.ds(1, doms, stride=2), :]
    for h in range(doms):
        sent_ref[ROWS * h + 16 : ROWS * h + 20, :] = row_ref[4 * h : 4 * h + 4, :].astype(BF16)
    moves[10].wait()


def first_stage(
    inverse, trace_map, panel_coupling, coupling, neighbours, iface_count, surface_rows, factor,
    colloc, quad_points, quad_weight, doms,
):
    shape = jax.ShapeDtypeStruct
    coupling = coupling.transpose(1, 0, 2)
    return pl.pallas_call(
        first_kernel,
        out_shape=(
            shape((ROWS * doms, LANE), BF16),
            shape(inverse.shape, BF16),
            shape(trace_map.shape, BF16),
            shape(panel_coupling.shape, BF16),
            shape(factor.shape, BF16),
            shape((doms, doms), BF16),
            shape((doms, LANE), F32),
        ),
        in_specs=[pl.BlockSpec(memory_space=pltpu.HBM)] * 11,
        out_specs=(VM,) * 7,
        scratch_shapes=[
            pltpu.VMEM(coupling.shape, F32),
            pltpu.SMEM(neighbours.shape, jnp.int32),
            pltpu.SMEM(iface_count.shape, jnp.int32),
            pltpu.VMEM(surface_rows.shape, jnp.int32),
            pltpu.VMEM(factor.shape, F32),
            pltpu.VMEM(colloc.shape, F32),
            pltpu.VMEM(quad_points.shape, F32),
            pltpu.VMEM(quad_weight.shape, F32),
            pltpu.VMEM((16, doms), F32),
            pltpu.VMEM((8, LIVE), F32),
            pltpu.VMEM((8, doms), F32),
            pltpu.VMEM((LIVE, LANE), F32),
            pltpu.VMEM((4 * doms, LANE), F32),
            pltpu.SemaphoreType.DMA((11,)),
        ],
        compiler_params=PARAMS,
        name="first_stage",
    )(
        *(
            pltpu.with_memory_space_constraint(x, pltpu.HBM)
            for x in (
                inverse, trace_map, panel_coupling, coupling, neighbours, iface_count, surface_rows,
                factor, colloc, quad_points, quad_weight,
            )
        )
    )


def mix_kernel(got_ref, pair_ref, block_hbm, sent_ref, picks_ref, block_ref, row_ref, sem):
    doms = pair_ref.shape[0]
    cols = sent_ref.shape[0]
    move = pltpu.make_async_copy(block_hbm, block_ref, sem.at[0])
    move.start()
    for h in range(doms):
        row_ref[4 * h : 4 * h + 4, :] = got_ref[ROWS * h + 16 : ROWS * h + 20, :].astype(F32)
    misc = row_ref[pl.ds(2, doms, stride=4), :]
    weights = misc + pltpu.roll(misc, LANE - 8, 1) + pltpu.roll(misc, LANE - 16, 1)
    sources = iota((doms, doms), 1).astype(F32)
    mixed = []
    for r in range(2):
        mixing = jnp.zeros((doms, doms), F32)
        for k in range(6):
            lane = 48 + 24 * r + k
            mixing = mixing + jnp.where(
                misc[:, 96 + k : 97 + k] == sources, weights[:, lane : lane + 1], 0.0
            )
        summed = jnp.dot(
            mixing,
            row_ref[pl.ds(r, doms, stride=4), :],
            precision=lax.Precision.HIGHEST,
            preferred_element_type=F32,
        )
        row = (2 * lax.axis_index("dom") + r).astype(F32)
        mixed.append(jnp.where(misc[:, 102:103] > row, summed, 0.0))
    row_ref[pl.ds(0, doms, stride=2), :] = mixed[0]
    row_ref[pl.ds(1, doms, stride=2), :] = mixed[1]
    correction = row_ref[: 2 * doms, :].astype(BF16)
    for c in range(cols):
        sent_ref[c] = correction
    move.wait()
    for p in range(NPAN):
        owner = lax.div(block_ref[p], cols)
        picks_ref[p] = pair_ref[pl.ds(owner, 1)][0]


def mix_stage(got, panel_block, doms, cols):
    return pl.pallas_call(
        mix_kernel,
        out_shape=(
            jax.ShapeDtypeStruct((cols, 2 * doms, LANE), BF16),
            jax.ShapeDtypeStruct((NPAN, ROWS // 2, 2, LANE), BF16),
        ),
        in_specs=[VM, VM, pl.BlockSpec(memory_space=pltpu.HBM)],
        out_specs=(VM, VM),
        scratch_shapes=[
            pltpu.SMEM(panel_block.shape, jnp.int32),
            pltpu.VMEM((4 * doms, LANE), F32),
            pltpu.SemaphoreType.DMA((1,)),
        ],
        compiler_params=PARAMS,
        name="mix_stage",
    )(
        got.reshape(ROWS * doms, LANE),
        got,
        pltpu.with_memory_space_constraint(panel_block, pltpu.HBM),
    )


def second_kernel(correction_ref, loads_ref, inv_ref, picks_ref, out_ref, loaded_ref):
    cols = correction_ref.shape[0]
    for c in range(cols):
        top = loads_ref[0, MB * c : MB * c + MAX_LIVE, :].astype(F32)
        top = top - correction_ref[c, :MAX_LIVE, :].astype(F32)
        loaded_ref[MB * c : MB * c + MAX_LIVE, :] = top.astype(BF16)
        loaded_ref[MB * c + MAX_LIVE : MB * (c + 1), :] = loads_ref[0, MB * c + MAX_LIVE : MB * (c + 1), :]
    second = jnp.dot(inv_ref[0], loaded_ref[...], preferred_element_type=F32)
    out_ref[:MB, :] = second.astype(BF16)
    out_ref[MB + 32 :, :] = jnp.zeros((16, LANE), BF16)
    for p in range(NPAN):
        out_ref[MB + 16 * p : MB + 16 * p + 16, :] = picks_ref[ROWS * p : ROWS * p + 16, :]
        out_ref[MB + 32 + 2 * p : MB + 34 + 2 * p, :] = picks_ref[ROWS * p + 18 : ROWS * p + 20, :]


def second_stage(correction, loads, inverse, picks):
    return pl.pallas_call(
        second_kernel,
        out_shape=jax.ShapeDtypeStruct((MB + 48, LANE), BF16),
        in_specs=[VM] * 4,
        out_specs=VM,
        scratch_shapes=[pltpu.VMEM(loads.shape[1:], BF16)],
        compiler_params=PARAMS,
        name="second_stage",
    )(correction, loads, inverse, picks.reshape(NPAN * ROWS, LANE))


def trace_kernel(
    gathered_ref, map_ref, block_hbm, shared_ref, last_ref, block_ref, second_ref, row_ref, sem
):
    move = pltpu.make_async_copy(block_hbm, block_ref, sem.at[0])
    move.start()
    cols = gathered_ref.shape[0]
    doms = map_ref.shape[1]
    core = lax.rem(lax.axis_index("col"), 2)
    for c in range(cols):
        second_ref[MB * c : MB * (c + 1), :] = gathered_ref[c, :MB, :]
    traces = jnp.dot(map_ref[0], second_ref[...], preferred_element_type=F32)
    move.wait()
    lanes = [lax.rem(block_ref[p], cols) for p in range(NPAN)]
    own = jnp.where(core == 0, lanes[0], lanes[1])
    first = gathered_ref[pl.ds(own, 1)][0, MB : MB + 16, :]
    second = gathered_ref[pl.ds(own, 1)][0, MB + 16 : MB + 32, :]
    shared_ref[...] = jnp.where(core == 0, first.astype(F32), second.astype(F32)).astype(BF16)
    quads = [
        gathered_ref[pl.ds(lanes[p], 1)][0, MB + 32 : MB + 48, :].astype(F32)[2 * p : 2 * p + 1, :]
        for p in range(NPAN)
    ]
    tail = jnp.where(iota((1, LANE), 1) < 48, quads[0], pltpu.roll(quads[1], 48, 1))
    row_ref[pl.ds(0, doms, stride=2), :] = traces
    row_ref[pl.ds(1, doms, stride=2), :] = jnp.broadcast_to(tail, (doms, LANE))
    last_ref[...] = row_ref[...].astype(BF16)


def trace_stage(gathered, trace_map, panel_block):
    doms = trace_map.shape[1]
    return pl.pallas_call(
        trace_kernel,
        out_shape=(
            jax.ShapeDtypeStruct((16, LANE), BF16),
            jax.ShapeDtypeStruct((2 * doms, LANE), BF16),
        ),
        in_specs=[VM, VM, pl.BlockSpec(memory_space=pltpu.HBM)],
        out_specs=(VM, VM),
        scratch_shapes=[
            pltpu.SMEM(panel_block.shape, jnp.int32),
            pltpu.VMEM((trace_map.shape[2], LANE), BF16),
            pltpu.VMEM((2 * doms, LANE), F32),
            pltpu.SemaphoreType.DMA((1,)),
        ],
        compiler_params=PARAMS,
        name="trace_stage",
    )(gathered, trace_map, pltpu.with_memory_space_constraint(panel_block, pltpu.HBM))


def panel_of(block_ref, panel_ref, doms):
    for h in range(doms):
        tile = block_ref[18 * h : 18 * h + 16, :]
        panel_ref[pl.ds(16 * (h // 16), 16), pl.ds(LANE * (h % 16), LANE)] = tile


def placed(low_ref, panel_ref, side):
    prior = lax.dot_general(
        low_ref[...], panel_ref[...], (((1,), (1,)), ((), ())), preferred_element_type=F32
    )
    both = jnp.concatenate([prior, prior], axis=1)
    return jnp.where((iota(both.shape, 1) >= P_SIZE) == (side == 1), both, 0.0)


def near_kernel(block_ref, low_ref, landing_ref, spots_ref, base_ref, panel_ref, row_ref):
    doms = landing_ref.shape[1]
    core = lax.rem(lax.axis_index("col"), 2)
    for h in range(doms):
        row_ref[2 * h : 2 * h + 2, :] = block_ref[18 * h + 16 : 18 * h + 18, :].astype(F32)
    traces = row_ref[pl.ds(0, doms, stride=2), :].astype(BF16)
    tails = row_ref[pl.ds(1, doms, stride=2), :]
    surface = jnp.dot(landing_ref[...], traces, preferred_element_type=F32)
    halves = []
    for p in range(NPAN):
        parts = []
        for t in range(3):
            pick = iota((16, LANE), 1) == iota((16, LANE), 0) + (48 * p + 16 * t)
            parts.append(turned(pick.astype(BF16), tails))
        halves.append((parts[2] + parts[1]) + parts[0])
    quads = jnp.concatenate(halves, axis=1)
    kernel_block = jnp.zeros_like(surface)
    for b in range(4):
        squared = jnp.zeros_like(surface)
        for c in range(3):
            shifted = spots_ref[:, c : c + 1] - quads[4 * c + b : 4 * c + b + 1, :]
            squared = squared + shifted * shifted
        green = jnp.cos(WAVE_NUMBER * jnp.sqrt(squared)) / (
            4.0 * math.pi * jnp.sqrt(squared + SMOOTHING * SMOOTHING)
        )
        kernel_block = kernel_block + quads[12 + b : 13 + b, :] * green
    panel_of(block_ref, panel_ref, doms)
    base_ref[...] = kernel_block - surface - placed(low_ref, panel_ref, core)


def far_kernel(block_ref, low_ref, base_ref, out_ref, panel_ref):
    core = lax.rem(lax.axis_index("col"), 2)
    panel_of(block_ref, panel_ref, block_ref.shape[0] // 18)
    out_ref[...] = base_ref[...] - placed(low_ref, panel_ref, 1 - core)


def near_stage(block, low, landing, spots):
    return pl.pallas_call(
        near_kernel,
        out_shape=jax.ShapeDtypeStruct((low.shape[0], LANE), F32),
        in_specs=[VM] * 4,
        out_specs=VM,
        scratch_shapes=[
            pltpu.VMEM(low.shape, BF16),
            pltpu.VMEM((2 * landing.shape[1], LANE), F32),
        ],
        compiler_params=PARAMS,
        cost_estimate=pl.CostEstimate(flops=40_000_000, bytes_accessed=1_000_000, transcendentals=100_000),
        name="near_stage",
    )(block, low, landing, spots)


def far_stage(block, low, base):
    return pl.pallas_call(
        far_kernel,
        out_shape=jax.ShapeDtypeStruct(base.shape, F32),
        in_specs=[VM] * 3,
        out_specs=VM,
        scratch_shapes=[pltpu.VMEM(low.shape, BF16)],
        compiler_params=PARAMS,
        name="far_stage",
    )(block, low, base)


def local(
    inverse,
    trace_map,
    panel_coupling,
    coupling,
    neighbours,
    iface_count,
    surface_rows,
    factor,
    colloc,
    quad_points,
    quad_weight,
    panel_block,
):
    doms = lax.axis_size("dom")
    cols = lax.axis_size("col")
    sent, inverse, trace_map, loads, factor_low, landing, spots = first_stage(
        inverse, trace_map, panel_coupling, coupling, neighbours, iface_count, surface_rows, factor,
        colloc, quad_points, quad_weight, doms,
    )
    got = lax.all_to_all(sent.reshape(doms, ROWS // 2, 2, LANE), "dom", 0, 0, tiled=True)
    sent, picks = mix_stage(got, panel_block, doms, cols)

    sent = sent.reshape(cols * doms, 2, LANE)
    correction = lax.all_to_all(sent, ("col", "dom"), 0, 0, tiled=True)
    correction = correction.reshape(cols, 2 * doms, LANE)
    pieces = second_stage(correction, loads, inverse, picks)
    gathered = lax.all_gather(pieces, "col", axis=0, tiled=False)
    shared, last = trace_stage(gathered, trace_map, panel_block)

    sent = jnp.concatenate(
        [
            jnp.broadcast_to(shared.reshape(1, 8, 2, LANE), (doms, 8, 2, LANE)),
            last.reshape(doms, 1, 2, LANE),
        ],
        axis=1,
    )
    got = lax.all_to_all(sent, "dom", 0, 0, tiled=True)
    other = lax.ppermute(got, "col", [(c, c ^ 1) for c in range(cols)])
    base = near_stage(got.reshape(18 * doms, LANE), factor_low, landing, spots)
    return far_stage(other.reshape(18 * doms, LANE), factor_low, base)


def solution(mesh):
    in_specs = (
        P("dom", "col", None),
        P("dom", "col", None),
        P("dom", None, None),
        P("dom", None, "col"),
        P("dom", None),
        P(),
        P("dom", "col", None, None),
        P(("dom", "col"), None),
        P(None, ("dom", "col")),
        P(None, None, ("dom", "col")),
        P(None, ("dom", "col")),
        P(),
    )
    out_specs = P(("dom", "col"), None)
    return jax.shard_map(local, mesh=mesh, in_specs=in_specs, out_specs=out_specs, check_vma=False)
```

time: 109 us -> 102 us (0.936)
  blocking collectives: 77.8 us -> 90.9 us
  waiting for transfers between devices: 11.5 us -> 0.29 us
  starting transfers between devices: 9.76 us -> 3.98 us
  local copies, waits for them, and re-layouts: 1.71 us -> 0.14 us
  other arithmetic: 1.83 us -> 0.39 us
  matrix products: 1.18 us -> 0 us
    all_to_all x0 -> x2, blocking collectives: none -> 58 us  [the longest x1 33.4 us: local(): correction = lax.all_to_all(sent, ('col', 'dom'), 0, 0, tiled=True)]
    all_to_all x2 -> x1, blocking collectives: 40 us -> 16.6 us  [local(): got = lax.all_to_all(sent, 'dom', 0, 0, tiled=True)]
    all_gather x1 -> x0, blocking collectives: 22.4 us -> none  [local(): correction = lax.all_gather(arrived[:MAX_LIVE], 'col', axis=0, tiled=False)]
    all_to_all x1 -> x0, waiting for transfers between devices: 11.5 us -> none  [local(): got = lax.all_to_all(sent, 'dom', 0, 0, tiled=True)]
    all_to_all x1 -> x0, starting transfers between devices: 5.77 us -> none  [local(): got = lax.all_to_all(sent, 'dom', 0, 0, tiled=True)]
    pallas_call x2 -> x4, Pallas kernels: 2.99 us -> 4.45 us  [the longest x1 1.9 us: first_stage(): pl.pallas_call(first_kernel, out_shape=(shape((ROWS * doms, LANE), BF16),...]
    dot_general x3 -> x0, matrix products: 1.18 us -> none  [the longest x1 0.75 us: local(): surface_sum = jnp.dot(landing, got[:, 8, 0], preferred_element_type=F32)]
  transfers between devices with their start and end apart: 2 -> 1, of which waited for: 1 -> 1; matrix products, arithmetic and copies ran while one was open for 1% -> 0% of each run, Pallas kernels for 0% -> 1%
where the time goes in v4:
time: 102 us; the launch traced here: 101 us
  blocking collectives  90.9 us (89%)
  Pallas kernels  5.7 us (6%)
  starting transfers between devices  3.98 us (4%)
    all_to_all x1, blocking collectives, local(): correction = lax.all_to_all(sent, ('col', 'dom'), 0, 0, tiled=True)  33.4 us
    all_to_all x1, blocking collectives, local(): lax.all_to_all(sent.reshape(doms, ROWS // 2, 2, LANE), 'dom', 0, 0, tiled...  24.6 us
    all_to_all x1, blocking collectives, local(): got = lax.all_to_all(sent, 'dom', 0, 0, tiled=True)  16.6 us
    all_gather x1, blocking collectives, local(): gathered = lax.all_gather(pieces, 'col', axis=0, tiled=False)  16.3 us
    ppermute x1, starting transfers between devices, local(): other = lax.ppermute(got, 'col', [(c, c ^ 1) for c in range(cols)])  3.98 us
  transfers between devices with their start and end apart: 1, of which 1 were waited for; matrix products, arithmetic and copies ran while one was open for 0% of the time, Pallas kernels for 1%

profile of v4, /device:TPU:1, one launch (start us, length us, event | category | flops | bytes accessed | tf_op | source)
XLA Modules:
  0.0 101.4 jit_solution(7425730493747929152)
XLA Ops:
  0.0 1.9 %first_stage.1 = (bf16[1280,128]{1,0:T(8,128)(2,1)S(1)}, bf16[1,208,1664]{2,1,0:T(8,128)(2,1)S(1)}, bf16[1,64,1664]{2,1,0:T(8,128)(2,1)S(1)}, bf16[1,1664,128]{2...) custom-call(bf16[1,208,1664]{2,1,0:T(8,128)(2,1)} %inv_hbm.1, ...), custom_call_target="tpu_custom_call" | custom-call | tf_op jit(solution)/shard_map/first_stage/pallas_call | solution.py:124
  1.9 24.6 %all_to_all.15.pair_ref = bf16[64,10,2,128]{3,2,1,0:T(2,128)(2,1)S(1)} all-to-all(bf16[64,10,2,128]{3,2,1,0:T(2,128)(2,1)S(1)} %bitcast.17), channel_id=1, replica_groups=mesh['dom'=64,'col'=8] {'dom'}, dimensions={0} | all-to-all | bytes 655360 | tf_op jit(solution)/shard_map/all_to_all | solution.py:399
  26.6 0.7 mix_stage.1
  27.3 33.4 %all_to_all.16 = bf16[512,2,128]{2,1,0:T(2,128)(2,1)S(1)} all-to-all(bf16[512,2,128]{2,1,0:T(2,128)(2,1)S(1)} %bitcast.19), channel_id=1, replica_groups=mesh['dom'=64,'col'=8] {'col','dom'}, dimensions={0} | all-to-all | bytes 524288 | tf_op jit(solution)/shard_map/all_to_all | solution.py:403
  60.6 0.4 second_stage.1
  61.0 16.3 %all-gather = bf16[2048,128]{1,0:T(8,128)(2,1)S(1)} all-gather(bf16[256,128]{1,0:T(8,128)(2,1)S(1)} %second_stage.1), channel_id=2, replica_groups=mesh['dom'=64,'col'=8] {'col'}, dimensions={0}, use_global_device_ids=true | all-gather | bytes 589824 | tf_op jit(solution)/shard_map/all_gather | solution.py:406
  77.3 0.8 trace_stage.1
  78.2 0.1 broadcast_in_dim.8
  78.3 0.4 pad_maximum_fusion
  78.7 16.6 %all_to_all.17 = bf16[64,9,2,128]{3,2,1,0:T(2,128)(2,1)S(1)} all-to-all(bf16[64,9,2,128]{3,2,1,0:T(2,128)(2,1)S(1)} %pad_maximum_fusion), channel_id=1, replica_groups=mesh['dom'=64,'col'=8] {'dom'}, dimensions={0} | all-to-all | bytes 589824 | tf_op jit(solution)/shard_map/all_to_all | solution.py:416
  95.3 4.0 %collective-permute-start = (bf16[64,9,2,128]{3,2,1,0:T(2,128)(2,1)S(1)}, bf16[64,9,2,128]{3,2,1,0:T(2,128)(2,1)S(1)}, u32[]{:S(2)}, u32[]{:S(2)}) collective-permute-start(bf16[64,9,2,128]{3,2,1,0:T(2,128)(2,1)S(1)} %all_to_all.17), channel_id=1, source_target_pairs={{0,1},{1,0},{2,3},{3,2},{4,5},{5,4},{6,7},{7,6},{8,9},{9,8},{10,11... | collective-permute-start | bytes 884744 | tf_op jit(solution)/shard_map/ppermute | solution.py:417
  99.3 0.9 near_stage.1.base_ref
  100.2 0.3 collective-permute-done
  100.5 1.0 far_stage.1
Async XLA Ops:
  95.3 5.2 %collective-permute-start = (bf16[64,9,2,128]{3,2,1,0:T(2,128)(2,1)S(1)}, bf16[64,9,2,128]{3,2,1,0:T(2,128)(2,1)S(1)}, u32[]{:S(2)}, u32[]{:S(2)}) collective-permute-start(bf16[64,9,2,128]{3,2,1,0:T(2,128)(2,1)S(1)} %all_to_all.17), channel_id=1, source_target_pairs={{0,1},{1,0},{2,3},{3,2},{4,5},{5,4},{6,7},{7,6},{8,9},{9,8},{10,11... | collective-permute-start | bytes 884744 | tf_op jit(solution)/shard_map/ppermute | solution.py:417

commit v5 on v4

--- a/solution.py
+++ b/solution.py
@@ -13,7 +13,8 @@
 LIVE = 128
 MAX_LIVE = 112
 LANE = 128
-ROWS = 20
+ROWS = 4
+PIECE = 224
 
 WAVE_NUMBER = 8.0
 SMOOTHING = 0.05
@@ -100,9 +101,6 @@
     spots_ref[...] = spots + pltpu.roll(spots, LANE - 8, 1) + pltpu.roll(spots, LANE - 16, 1)
     landing_ref[...] = (iota((doms, doms), 0) == rows_ref[0, 0]).astype(BF16)
     moves[7].wait()
-    for h in range(doms):
-        tile = factor_ref[pl.ds(16 * (h // 16), 16), pl.ds(LANE * (h % 16), LANE)]
-        sent_ref[ROWS * h : ROWS * h + 16, :] = tile.astype(BF16)
     low_ref[...] = factor_ref[...].astype(BF16)
     for move in moves[8:10]:
         move.wait()
@@ -110,8 +108,7 @@
     first_ref[...] = jnp.where(iota((LIVE, LANE), 0) < count, first, 0.0)
     row_ref[pl.ds(0, doms, stride=4), :] = first_ref[pl.ds(0, doms, stride=2), :]
     row_ref[pl.ds(1, doms, stride=4), :] = first_ref[pl.ds(1, doms, stride=2), :]
-    for h in range(doms):
-        sent_ref[ROWS * h + 16 : ROWS * h + 20, :] = row_ref[4 * h : 4 * h + 4, :].astype(BF16)
+    sent_ref[...] = row_ref[...].astype(BF16)
     moves[10].wait()
 
 
@@ -163,17 +160,18 @@
     )
 
 
-def mix_kernel(got_ref, pair_ref, block_hbm, sent_ref, picks_ref, block_ref, row_ref, sem):
+def mix_kernel(got_ref, pair_ref, low_ref, block_hbm, sent_ref, quad_ref, block_ref, row_ref, work_ref, sem):
     doms = pair_ref.shape[0]
-    cols = sent_ref.shape[0]
+    cols = sent_ref.shape[0] // (ROWS * doms)
     move = pltpu.make_async_copy(block_hbm, block_ref, sem.at[0])
     move.start()
-    for h in range(doms):
-        row_ref[4 * h : 4 * h + 4, :] = got_ref[ROWS * h + 16 : ROWS * h + 20, :].astype(F32)
-    misc = row_ref[pl.ds(2, doms, stride=4), :]
+    row_ref[...] = got_ref[...].astype(F32)
+    for t in range(2 * doms):
+        tile = low_ref[pl.ds(8 * (t // 16), 8), pl.ds(LANE * (t % 16), LANE)]
+        work_ref[pl.ds(ROWS * (t // 2) + 2 + t % 2, cols, stride=ROWS * doms), :] = tile.astype(F32)
+    misc = row_ref[pl.ds(2, doms, stride=ROWS), :]
     weights = misc + pltpu.roll(misc, LANE - 8, 1) + pltpu.roll(misc, LANE - 16, 1)
     sources = iota((doms, doms), 1).astype(F32)
-    mixed = []
     for r in range(2):
         mixing = jnp.zeros((doms, doms), F32)
         for k in range(6):
@@ -183,35 +181,34 @@
             )
         summed = jnp.dot(
             mixing,
-            row_ref[pl.ds(r, doms, stride=4), :],
+            row_ref[pl.ds(r, doms, stride=ROWS), :],
             precision=lax.Precision.HIGHEST,
             preferred_element_type=F32,
         )
         row = (2 * lax.axis_index("dom") + r).astype(F32)
-        mixed.append(jnp.where(misc[:, 102:103] > row, summed, 0.0))
-    row_ref[pl.ds(0, doms, stride=2), :] = mixed[0]
-    row_ref[pl.ds(1, doms, stride=2), :] = mixed[1]
-    correction = row_ref[: 2 * doms, :].astype(BF16)
-    for c in range(cols):
-        sent_ref[c] = correction
+        summed = jnp.where(misc[:, 102:103] > row, summed, 0.0)
+        for c in range(cols):
+            work_ref[pl.ds(ROWS * doms * c + r, doms, stride=ROWS), :] = summed
+    sent_ref[...] = work_ref[...].astype(BF16)
     move.wait()
     for p in range(NPAN):
         owner = lax.div(block_ref[p], cols)
-        picks_ref[p] = pair_ref[pl.ds(owner, 1)][0]
-
-
-def mix_stage(got, panel_block, doms, cols):
+        quad_ref[p] = pair_ref[pl.ds(owner, 1)][0, 1]
+
+
+def mix_stage(got, low, panel_block, doms, cols):
     return pl.pallas_call(
         mix_kernel,
         out_shape=(
-            jax.ShapeDtypeStruct((cols, 2 * doms, LANE), BF16),
-            jax.ShapeDtypeStruct((NPAN, ROWS // 2, 2, LANE), BF16),
+            jax.ShapeDtypeStruct((ROWS * doms * cols, LANE), BF16),
+            jax.ShapeDtypeStruct((NPAN, 2, LANE), BF16),
         ),
-        in_specs=[VM, VM, pl.BlockSpec(memory_space=pltpu.HBM)],
+        in_specs=[VM, VM, VM, pl.BlockSpec(memory_space=pltpu.HBM)],
         out_specs=(VM, VM),
         scratch_shapes=[
             pltpu.SMEM(panel_block.shape, jnp.int32),
-            pltpu.VMEM((4 * doms, LANE), F32),
+            pltpu.VMEM((ROWS * doms, LANE), F32),
+            pltpu.VMEM((ROWS * doms * cols, LANE), F32),
             pltpu.SemaphoreType.DMA((1,)),
         ],
         compiler_params=PARAMS,
@@ -219,39 +216,62 @@
     )(
         got.reshape(ROWS * doms, LANE),
         got,
+        low,
         pltpu.with_memory_space_constraint(panel_block, pltpu.HBM),
     )
 
 
-def second_kernel(correction_ref, loads_ref, inv_ref, picks_ref, out_ref, loaded_ref):
-    cols = correction_ref.shape[0]
+def second_kernel(
+    got_ref, pair_ref, loads_ref, inv_ref, quad_ref, block_hbm, out_ref, block_ref, work_ref, loaded_ref, sem
+):
+    cols = lax.axis_size("col")
+    doms = pair_ref.shape[0] // cols
+    move = pltpu.make_async_copy(block_hbm, block_ref, sem.at[0])
+    move.start()
+    loaded_ref[...] = loads_ref[0].astype(F32)
+    work_ref[...] = got_ref[...].astype(F32)
     for c in range(cols):
-        top = loads_ref[0, MB * c : MB * c + MAX_LIVE, :].astype(F32)
-        top = top - correction_ref[c, :MAX_LIVE, :].astype(F32)
-        loaded_ref[MB * c : MB * c + MAX_LIVE, :] = top.astype(BF16)
-        loaded_ref[MB * c + MAX_LIVE : MB * (c + 1), :] = loads_ref[0, MB * c + MAX_LIVE : MB * (c + 1), :]
-    second = jnp.dot(inv_ref[0], loaded_ref[...], preferred_element_type=F32)
+        for r in range(2):
+            rows = pl.ds(MB * c + r, MAX_LIVE // 2, stride=2)
+            correction = work_ref[pl.ds(ROWS * doms * c + r, MAX_LIVE // 2, stride=ROWS), :]
+            loaded_ref[rows, :] = loaded_ref[rows, :] - correction
+    second = jnp.dot(inv_ref[0], loaded_ref[...].astype(BF16), preferred_element_type=F32)
     out_ref[:MB, :] = second.astype(BF16)
-    out_ref[MB + 32 :, :] = jnp.zeros((16, LANE), BF16)
+    out_ref[MB:, :] = jnp.zeros((PIECE - MB, LANE), BF16)
+    move.wait()
     for p in range(NPAN):
-        out_ref[MB + 16 * p : MB + 16 * p + 16, :] = picks_ref[ROWS * p : ROWS * p + 16, :]
-        out_ref[MB + 32 + 2 * p : MB + 34 + 2 * p, :] = picks_ref[ROWS * p + 18 : ROWS * p + 20, :]
-
-
-def second_stage(correction, loads, inverse, picks):
+        owner = lax.rem(block_ref[p], cols) * doms + lax.div(block_ref[p], cols)
+        out_ref[MB + 2 * p : MB + 2 * p + 2, :] = pair_ref[pl.ds(owner, 1)][0, 1]
+        out_ref[MB + 4 + 2 * p : MB + 6 + 2 * p, :] = quad_ref[p]
+
+
+def second_stage(got, loads, inverse, quads, panel_block):
     return pl.pallas_call(
         second_kernel,
-        out_shape=jax.ShapeDtypeStruct((MB + 48, LANE), BF16),
-        in_specs=[VM] * 4,
+        out_shape=jax.ShapeDtypeStruct((PIECE, LANE), BF16),
+        in_specs=[VM] * 5 + [pl.BlockSpec(memory_space=pltpu.HBM)],
         out_specs=VM,
-        scratch_shapes=[pltpu.VMEM(loads.shape[1:], BF16)],
+        scratch_shapes=[
+            pltpu.SMEM(panel_block.shape, jnp.int32),
+            pltpu.VMEM((2 * got.shape[0] * 2, LANE), F32),
+            pltpu.VMEM(loads.shape[1:], F32),
+            pltpu.SemaphoreType.DMA((1,)),
+        ],
         compiler_params=PARAMS,
         name="second_stage",
-    )(correction, loads, inverse, picks.reshape(NPAN * ROWS, LANE))
+    )(
+        got.reshape(-1, LANE),
+        got,
+        loads,
+        inverse,
+        quads,
+        pltpu.with_memory_space_constraint(panel_block, pltpu.HBM),
+    )
 
 
 def trace_kernel(
-    gathered_ref, map_ref, block_hbm, shared_ref, last_ref, block_ref, second_ref, row_ref, sem
+    gathered_ref, pair_ref, map_ref, block_hbm, shared_ref, last_ref, block_ref, second_ref, row_ref,
+    tile_ref, sem
 ):
     move = pltpu.make_async_copy(block_hbm, block_ref, sem.at[0])
     move.start()
@@ -260,17 +280,16 @@
     core = lax.rem(lax.axis_index("col"), 2)
     for c in range(cols):
         second_ref[MB * c : MB * (c + 1), :] = gathered_ref[c, :MB, :]
+        tile_ref[2 * c : 2 * c + 2, :] = pair_ref[c, pl.ds(MB // 2 + core, 1)][0].astype(F32)
     traces = jnp.dot(map_ref[0], second_ref[...], preferred_element_type=F32)
+    tiles = [tile_ref[pl.ds(r, cols, stride=2), :] for r in range(2)]
+    shared_ref[...] = jnp.concatenate(tiles, axis=0).astype(BF16)
     move.wait()
-    lanes = [lax.rem(block_ref[p], cols) for p in range(NPAN)]
-    own = jnp.where(core == 0, lanes[0], lanes[1])
-    first = gathered_ref[pl.ds(own, 1)][0, MB : MB + 16, :]
-    second = gathered_ref[pl.ds(own, 1)][0, MB + 16 : MB + 32, :]
-    shared_ref[...] = jnp.where(core == 0, first.astype(F32), second.astype(F32)).astype(BF16)
-    quads = [
-        gathered_ref[pl.ds(lanes[p], 1)][0, MB + 32 : MB + 48, :].astype(F32)[2 * p : 2 * p + 1, :]
-        for p in range(NPAN)
-    ]
+    quads = []
+    for p in range(NPAN):
+        lane = lax.rem(block_ref[p], cols)
+        rows = gathered_ref[pl.ds(lane, 1)][0, MB : MB + 16, :].astype(F32)
+        quads.append(rows[4 + 2 * p : 5 + 2 * p, :])
     tail = jnp.where(iota((1, LANE), 1) < 48, quads[0], pltpu.roll(quads[1], 48, 1))
     row_ref[pl.ds(0, doms, stride=2), :] = traces
     row_ref[pl.ds(1, doms, stride=2), :] = jnp.broadcast_to(tail, (doms, LANE))
@@ -285,23 +304,24 @@
             jax.ShapeDtypeStruct((16, LANE), BF16),
             jax.ShapeDtypeStruct((2 * doms, LANE), BF16),
         ),
-        in_specs=[VM, VM, pl.BlockSpec(memory_space=pltpu.HBM)],
+        in_specs=[VM, VM, VM, pl.BlockSpec(memory_space=pltpu.HBM)],
         out_specs=(VM, VM),
         scratch_shapes=[
             pltpu.SMEM(panel_block.shape, jnp.int32),
             pltpu.VMEM((trace_map.shape[2], LANE), BF16),
             pltpu.VMEM((2 * doms, LANE), F32),
+            pltpu.VMEM((16, LANE), F32),
             pltpu.SemaphoreType.DMA((1,)),
         ],
         compiler_params=PARAMS,
         name="trace_stage",
-    )(gathered, trace_map, pltpu.with_memory_space_constraint(panel_block, pltpu.HBM))
+    )(gathered, gathered.reshape(-1, PIECE // 2, 2, LANE), trace_map, pltpu.with_memory_space_constraint(panel_block, pltpu.HBM))
 
 
 def panel_of(block_ref, panel_ref, doms):
-    for h in range(doms):
-        tile = block_ref[18 * h : 18 * h + 16, :]
-        panel_ref[pl.ds(16 * (h // 16), 16), pl.ds(LANE * (h % 16), LANE)] = tile
+    for t in range(2 * doms):
+        tile = block_ref[18 * (t // 2) + 8 * (t % 2) : 18 * (t // 2) + 8 * (t % 2) + 8, :]
+        panel_ref[pl.ds(8 * (t // 16), 8), pl.ds(LANE * (t % 16), LANE)] = tile
 
 
 def placed(low_ref, panel_ref, side):
@@ -397,12 +417,11 @@
         colloc, quad_points, quad_weight, doms,
     )
     got = lax.all_to_all(sent.reshape(doms, ROWS // 2, 2, LANE), "dom", 0, 0, tiled=True)
-    sent, picks = mix_stage(got, panel_block, doms, cols)
-
-    sent = sent.reshape(cols * doms, 2, LANE)
-    correction = lax.all_to_all(sent, ("col", "dom"), 0, 0, tiled=True)
-    correction = correction.reshape(cols, 2 * doms, LANE)
-    pieces = second_stage(correction, loads, inverse, picks)
+    sent, quads = mix_stage(got, factor_low, panel_block, doms, cols)
+
+    sent = sent.reshape(cols * doms, 2, 2, LANE)
+    got = lax.all_to_all(sent, ("col", "dom"), 0, 0, tiled=True)
+    pieces = second_stage(got, loads, inverse, quads, panel_block)
     gathered = lax.all_gather(pieces, "col", axis=0, tiled=False)
     shared, last = trace_stage(gathered, trace_map, panel_block)
 

time: 102 us -> 103 us (level)
  Pallas kernels: 5.7 us -> 6.92 us
    all_to_all x1, blocking collectives: 33.4 us -> 36.8 us  [local(): got = lax.all_to_all(sent, ('col', 'dom'), 0, 0, tiled=True)]
    all_to_all x1, blocking collectives: 24.6 us -> 22 us  [local(): lax.all_to_all(sent.reshape(doms, ROWS // 2, 2, LANE), 'dom', 0, 0, tiled...]
    pallas_call x2, Pallas kernels: 1.1 us -> 2.39 us  [the longest x1 1.36 us: mix_stage(): pl.pallas_call(mix_kernel, out_shape=(jax.ShapeDtypeStruct((ROWS * doms *...]
where the time goes in v5:
time: 103 us
  blocking collectives  91.1 us (88%)
  Pallas kernels  6.92 us (7%)
  starting transfers between devices  3.99 us (4%)
    all_to_all x1, blocking collectives, local(): got = lax.all_to_all(sent, ('col', 'dom'), 0, 0, tiled=True)  36.8 us
    all_to_all x1, blocking collectives, local(): lax.all_to_all(sent.reshape(doms, ROWS // 2, 2, LANE), 'dom', 0, 0, tiled...  22 us
    all_to_all x1, blocking collectives, local(): got = lax.all_to_all(sent, 'dom', 0, 0, tiled=True)  17 us
    all_gather x1, blocking collectives, local(): gathered = lax.all_gather(pieces, 'col', axis=0, tiled=False)  15.3 us
    ppermute x1, starting transfers between devices, local(): other = lax.ppermute(got, 'col', [(c, c ^ 1) for c in range(cols)])  3.99 us
  transfers between devices with their start and end apart: 1, of which 1 were waited for; matrix products, arithmetic and copies ran while one was open for 0% of the time, Pallas kernels for 1%

profile of v5, /device:TPU:1, one launch (start us, length us, event | category | flops | bytes accessed | tf_op | source)
XLA Modules:
  0.0 102.8 jit_solution(1488488294971530072)
XLA Ops:
  0.0 1.9 %first_stage.1 = (bf16[256,128]{1,0:T(8,128)(2,1)S(1)}, bf16[1,208,1664]{2,1,0:T(8,128)(2,1)S(1)}, bf16[1,64,1664]{2,1,0:T(8,128)(2,1)S(1)}, bf16[1,1664,128]{2,...) custom-call(bf16[1,208,1664]{2,1,0:T(8,128)(2,1)} %inv_hbm.1, ...), custom_call_target="tpu_custom_call" | custom-call | tf_op jit(solution)/shard_map/first_stage/pallas_call | solution.py:121
  1.9 22.0 %all_to_all.15.pair_ref = bf16[64,2,2,128]{3,2,1,0:T(2,128)(2,1)S(1)} all-to-all(bf16[64,2,2,128]{3,2,1,0:T(2,128)(2,1)S(1)} %bitcast.20), channel_id=1, replica_groups=mesh['dom'=64,'col'=8] {'dom'}, dimensions={0} | all-to-all | bytes 131072 | tf_op jit(solution)/shard_map/all_to_all | solution.py:419
  23.9 1.4 %mix_stage.1 = (bf16[2048,128]{1,0:T(8,128)(2,1)S(1)}, bf16[2,2,128]{2,1,0:T(2,128)(2,1)S(1)}) custom-call(bf16[256,128]{1,0:T(8,128)(2,1)S(1)} %bitcast.17, bf16[64,2,2,128]{3,2,1,0:T(2,128)(2,1)S(1)} %all_to_all.15.pair_ref, bf16[64,2048]{1,0:T(8,128)(2,1)S(1)} %get-tuple-element.17.low_ref, s32[2]{0:T(128)} %block_hbm.5), custom_call_target="tpu_custom_call" | custom-call | tf_op jit(solution)/shard_map/mix_stage/pallas_call | solution.py:200
  25.3 36.8 %all_to_all.16.pair_ref = bf16[512,2,2,128]{3,2,1,0:T(2,128)(2,1)S(1)} all-to-all(bf16[512,2,2,128]{3,2,1,0:T(2,128)(2,1)S(1)} %bitcast.18), channel_id=1, replica_groups=mesh['dom'=64,'col'=8] {'col','dom'}, dimensions={0} | all-to-all | bytes 1048576 | tf_op jit(solution)/shard_map/all_to_all | solution.py:423
  62.0 1.0 second_stage.1
  63.1 15.3 %all-gather = bf16[1792,128]{1,0:T(8,128)(2,1)S(1)} all-gather(bf16[224,128]{1,0:T(8,128)(2,1)S(1)} %second_stage.1), channel_id=2, replica_groups=mesh['dom'=64,'col'=8] {'col'}, dimensions={0}, use_global_device_ids=true | all-gather | bytes 516096 | tf_op jit(solution)/shard_map/all_gather | solution.py:425
  78.4 0.8 trace_stage.1
  79.1 0.1 broadcast_in_dim.8
  79.3 0.4 pad_maximum_fusion
  79.7 17.0 %all_to_all.17 = bf16[64,9,2,128]{3,2,1,0:T(2,128)(2,1)S(1)} all-to-all(bf16[64,9,2,128]{3,2,1,0:T(2,128)(2,1)S(1)} %pad_maximum_fusion), channel_id=1, replica_groups=mesh['dom'=64,'col'=8] {'dom'}, dimensions={0} | all-to-all | bytes 589824 | tf_op jit(solution)/shard_map/all_to_all | solution.py:435
  96.7 4.0 %collective-permute-start = (bf16[64,9,2,128]{3,2,1,0:T(2,128)(2,1)S(1)}, bf16[64,9,2,128]{3,2,1,0:T(2,128)(2,1)S(1)}, u32[]{:S(2)}, u32[]{:S(2)}) collective-permute-start(bf16[64,9,2,128]{3,2,1,0:T(2,128)(2,1)S(1)} %all_to_all.17), channel_id=1, source_target_pairs={{0,1},{1,0},{2,3},{3,2},{4,5},{5,4},{6,7},{7,6},{8,9},{9,8},{10,11... | collective-permute-start | bytes 884744 | tf_op jit(solution)/shard_map/ppermute | solution.py:436
  100.7 0.9 near_stage.1.base_ref
  101.6 0.3 collective-permute-done
  101.9 1.0 far_stage.1
Async XLA Ops:
  96.7 5.2 %collective-permute-start = (bf16[64,9,2,128]{3,2,1,0:T(2,128)(2,1)S(1)}, bf16[64,9,2,128]{3,2,1,0:T(2,128)(2,1)S(1)}, u32[]{:S(2)}, u32[]{:S(2)}) collective-permute-start(bf16[64,9,2,128]{3,2,1,0:T(2,128)(2,1)S(1)} %all_to_all.17), channel_id=1, source_target_pairs={{0,1},{1,0},{2,3},{3,2},{4,5},{5,4},{6,7},{7,6},{8,9},{9,8},{10,11... | collective-permute-start | bytes 884744 | tf_op jit(solution)/shard_map/ppermute | solution.py:436

commit v6 on v4

--- a/solution.py
+++ b/solution.py
@@ -5,6 +5,7 @@
 from jax import lax
 from jax.experimental import pallas as pl
 from jax.experimental.pallas import tpu as pltpu
+from jax.sharding import Mesh
 from jax.sharding import PartitionSpec as P
 
 MB = 208
@@ -165,7 +166,8 @@
 
 def mix_kernel(got_ref, pair_ref, block_hbm, sent_ref, picks_ref, block_ref, row_ref, sem):
     doms = pair_ref.shape[0]
-    cols = sent_ref.shape[0]
+    copies = sent_ref.shape[0]
+    cols = 2 * copies
     move = pltpu.make_async_copy(block_hbm, block_ref, sem.at[0])
     move.start()
     for h in range(doms):
@@ -192,19 +194,19 @@
     row_ref[pl.ds(0, doms, stride=2), :] = mixed[0]
     row_ref[pl.ds(1, doms, stride=2), :] = mixed[1]
     correction = row_ref[: 2 * doms, :].astype(BF16)
-    for c in range(cols):
-        sent_ref[c] = correction
+    for z in range(copies):
+        sent_ref[z] = correction
     move.wait()
     for p in range(NPAN):
         owner = lax.div(block_ref[p], cols)
         picks_ref[p] = pair_ref[pl.ds(owner, 1)][0]
 
 
-def mix_stage(got, panel_block, doms, cols):
+def mix_stage(got, panel_block, doms, copies):
     return pl.pallas_call(
         mix_kernel,
         out_shape=(
-            jax.ShapeDtypeStruct((cols, 2 * doms, LANE), BF16),
+            jax.ShapeDtypeStruct((copies, 2 * doms, LANE), BF16),
             jax.ShapeDtypeStruct((NPAN, ROWS // 2, 2, LANE), BF16),
         ),
         in_specs=[VM, VM, pl.BlockSpec(memory_space=pltpu.HBM)],
@@ -223,11 +225,13 @@
     )
 
 
-def second_kernel(correction_ref, loads_ref, inv_ref, picks_ref, out_ref, loaded_ref):
-    cols = correction_ref.shape[0]
-    for c in range(cols):
-        top = loads_ref[0, MB * c : MB * c + MAX_LIVE, :].astype(F32)
-        top = top - correction_ref[c, :MAX_LIVE, :].astype(F32)
+def second_kernel(own_ref, other_ref, loads_ref, inv_ref, picks_ref, out_ref, loaded_ref):
+    first_core = lax.axis_index("core") == 0
+    for c in range(2 * own_ref.shape[0]):
+        own = own_ref[c // 2, :MAX_LIVE, :].astype(F32)
+        other = other_ref[c // 2, :MAX_LIVE, :].astype(F32)
+        correction = jnp.where(first_core == (c % 2 == 0), own, other)
+        top = loads_ref[0, MB * c : MB * c + MAX_LIVE, :].astype(F32) - correction
         loaded_ref[MB * c : MB * c + MAX_LIVE, :] = top.astype(BF16)
         loaded_ref[MB * c + MAX_LIVE : MB * (c + 1), :] = loads_ref[0, MB * c + MAX_LIVE : MB * (c + 1), :]
     second = jnp.dot(inv_ref[0], loaded_ref[...], preferred_element_type=F32)
@@ -238,16 +242,16 @@
         out_ref[MB + 32 + 2 * p : MB + 34 + 2 * p, :] = picks_ref[ROWS * p + 18 : ROWS * p + 20, :]
 
 
-def second_stage(correction, loads, inverse, picks):
+def second_stage(own, other, loads, inverse, picks):
     return pl.pallas_call(
         second_kernel,
         out_shape=jax.ShapeDtypeStruct((MB + 48, LANE), BF16),
-        in_specs=[VM] * 4,
+        in_specs=[VM] * 5,
         out_specs=VM,
         scratch_shapes=[pltpu.VMEM(loads.shape[1:], BF16)],
         compiler_params=PARAMS,
         name="second_stage",
-    )(correction, loads, inverse, picks.reshape(NPAN * ROWS, LANE))
+    )(own, other, loads, inverse, picks.reshape(NPAN * ROWS, LANE))
 
 
 def trace_kernel(
@@ -257,7 +261,7 @@
     move.start()
     cols = gathered_ref.shape[0]
     doms = map_ref.shape[1]
-    core = lax.rem(lax.axis_index("col"), 2)
+    core = lax.axis_index("core")
     for c in range(cols):
         second_ref[MB * c : MB * (c + 1), :] = gathered_ref[c, :MB, :]
     traces = jnp.dot(map_ref[0], second_ref[...], preferred_element_type=F32)
@@ -314,7 +318,7 @@
 
 def near_kernel(block_ref, low_ref, landing_ref, spots_ref, base_ref, panel_ref, row_ref):
     doms = landing_ref.shape[1]
-    core = lax.rem(lax.axis_index("col"), 2)
+    core = lax.axis_index("core")
     for h in range(doms):
         row_ref[2 * h : 2 * h + 2, :] = block_ref[18 * h + 16 : 18 * h + 18, :].astype(F32)
     traces = row_ref[pl.ds(0, doms, stride=2), :].astype(BF16)
@@ -343,7 +347,7 @@
 
 
 def far_kernel(block_ref, low_ref, base_ref, out_ref, panel_ref):
-    core = lax.rem(lax.axis_index("col"), 2)
+    core = lax.axis_index("core")
     panel_of(block_ref, panel_ref, block_ref.shape[0] // 18)
     out_ref[...] = base_ref[...] - placed(low_ref, panel_ref, 1 - core)
 
@@ -391,19 +395,20 @@
     panel_block,
 ):
     doms = lax.axis_size("dom")
-    cols = lax.axis_size("col")
+    levels = lax.axis_size("zh")
     sent, inverse, trace_map, loads, factor_low, landing, spots = first_stage(
         inverse, trace_map, panel_coupling, coupling, neighbours, iface_count, surface_rows, factor,
         colloc, quad_points, quad_weight, doms,
     )
     got = lax.all_to_all(sent.reshape(doms, ROWS // 2, 2, LANE), "dom", 0, 0, tiled=True)
-    sent, picks = mix_stage(got, panel_block, doms, cols)
-
-    sent = sent.reshape(cols * doms, 2, LANE)
-    correction = lax.all_to_all(sent, ("col", "dom"), 0, 0, tiled=True)
-    correction = correction.reshape(cols, 2 * doms, LANE)
-    pieces = second_stage(correction, loads, inverse, picks)
-    gathered = lax.all_gather(pieces, "col", axis=0, tiled=False)
+    sent, picks = mix_stage(got, panel_block, doms, levels)
+
+    sent = sent.reshape(levels * doms, 2, LANE)
+    own = lax.all_to_all(sent, ("zh", "dom"), 0, 0, tiled=True)
+    own = own.reshape(levels, 2 * doms, LANE)
+    other = lax.ppermute(own, "core", [(0, 1), (1, 0)])
+    pieces = second_stage(own, other, loads, inverse, picks)
+    gathered = lax.all_gather(pieces, ("zh", "core"), axis=0, tiled=False)
     shared, last = trace_stage(gathered, trace_map, panel_block)
 
     sent = jnp.concatenate(
@@ -414,25 +419,28 @@
         axis=1,
     )
     got = lax.all_to_all(sent, "dom", 0, 0, tiled=True)
-    other = lax.ppermute(got, "col", [(c, c ^ 1) for c in range(cols)])
+    other = lax.ppermute(got, "core", [(0, 1), (1, 0)])
     base = near_stage(got.reshape(18 * doms, LANE), factor_low, landing, spots)
     return far_stage(other.reshape(18 * doms, LANE), factor_low, base)
 
 
 def solution(mesh):
+    split = Mesh(mesh.devices.reshape(mesh.shape["dom"], -1, 2), ("dom", "zh", "core"))
+    col = ("zh", "core")
+    rows = ("dom", "zh", "core")
     in_specs = (
-        P("dom", "col", None),
-        P("dom", "col", None),
+        P("dom", col, None),
+        P("dom", col, None),
         P("dom", None, None),
-        P("dom", None, "col"),
+        P("dom", None, col),
         P("dom", None),
         P(),
-        P("dom", "col", None, None),
-        P(("dom", "col"), None),
-        P(None, ("dom", "col")),
-        P(None, None, ("dom", "col")),
-        P(None, ("dom", "col")),
+        P("dom", col, None, None),
+        P(rows, None),
+        P(None, rows),
+        P(None, None, rows),
+        P(None, rows),
         P(),
     )
-    out_specs = P(("dom", "col"), None)
-    return jax.shard_map(local, mesh=mesh, in_specs=in_specs, out_specs=out_specs, check_vma=False)
+    out_specs = P(rows, None)
+    return jax.shard_map(local, mesh=split, in_specs=in_specs, out_specs=out_specs, check_vma=False)

time: 102 us -> 103 us (level)
  starting transfers between devices: 3.98 us -> 8.59 us
  blocking collectives: 90.9 us -> 86.4 us
    ppermute x1 -> x2, starting transfers between devices: 3.98 us -> 8.59 us  [the longest x1 4.86 us: local(): other = lax.ppermute(own, 'core', [(0, 1), (1, 0)])]
    all_to_all x1, blocking collectives: 33.4 us -> 30.2 us  [local(): own = lax.all_to_all(sent, ('zh', 'dom'), 0, 0, tiled=True)]
  transfers between devices with their start and end apart: 1 -> 2, of which waited for: 1 -> 2; matrix products, arithmetic and copies ran while one was open for 0% -> 0% of each run, Pallas kernels for 1% -> 1%
where the time goes in v6:
time: 103 us
  blocking collectives  86.4 us (84%)
  starting transfers between devices  8.59 us (8%)
  Pallas kernels  5.7 us (6%)
  waiting for transfers between devices  1.25 us (1%)
    all_to_all x1, blocking collectives, local(): own = lax.all_to_all(sent, ('zh', 'dom'), 0, 0, tiled=True)  30.2 us
    all_to_all x1, blocking collectives, local(): lax.all_to_all(sent.reshape(doms, ROWS // 2, 2, LANE), 'dom', 0, 0, tiled...  24.6 us
    all_to_all x1, blocking collectives, local(): got = lax.all_to_all(sent, 'dom', 0, 0, tiled=True)  15.8 us
    all_gather x1, blocking collectives, local(): gathered = lax.all_gather(pieces, ('zh', 'core'), axis=0, tiled=False)  15.8 us
    ppermute x1, starting transfers between devices, local(): other = lax.ppermute(own, 'core', [(0, 1), (1, 0)])  4.86 us
    ppermute x1, starting transfers between devices, local(): other = lax.ppermute(got, 'core', [(0, 1), (1, 0)])  3.73 us
  transfers between devices with their start and end apart: 2, of which 2 were waited for; matrix products, arithmetic and copies ran while one was open for 0% of the time, Pallas kernels for 1%

profile of v6, /device:TPU:1, one launch (start us, length us, event | category | flops | bytes accessed | tf_op | source)
XLA Modules:
  0.0 102.6 jit_solution(1383707776813129223)
XLA Ops:
  0.0 1.9 %first_stage.1 = (bf16[1280,128]{1,0:T(8,128)(2,1)S(1)}, bf16[1,208,1664]{2,1,0:T(8,128)(2,1)S(1)}, bf16[1,64,1664]{2,1,0:T(8,128)(2,1)S(1)}, bf16[1,1664,128]{2...) custom-call(bf16[1,208,1664]{2,1,0:T(8,128)(2,1)} %inv_hbm.1, ...), custom_call_target="tpu_custom_call" | custom-call | tf_op jit(solution)/shard_map/first_stage/pallas_call | solution.py:125
  1.9 24.6 %all_to_all.15.pair_ref = bf16[64,10,2,128]{3,2,1,0:T(2,128)(2,1)S(1)} all-to-all(bf16[64,10,2,128]{3,2,1,0:T(2,128)(2,1)S(1)} %bitcast.18), channel_id=1, replica_groups=mesh['dom'=64,'zh'=4,'core'=2] {'dom'}, dimensions={0} | all-to-all | bytes 655360 | tf_op jit(solution)/shard_map/all_to_all | solution.py:403
  26.6 0.7 mix_stage.1
  27.3 30.2 %all_to_all.16 = bf16[256,2,128]{2,1,0:T(2,128)(2,1)S(1)} all-to-all(bf16[256,2,128]{2,1,0:T(2,128)(2,1)S(1)} %bitcast.20), channel_id=1, replica_groups=mesh['dom'=64,'zh'=4,'core'=2] {'zh','dom'}, dimensions={0} | all-to-all | bytes 262144 | tf_op jit(solution)/shard_map/all_to_all | solution.py:407
  57.5 4.9 %collective-permute-start = (bf16[4,128,128]{2,1,0:T(8,128)(2,1)S(1)}, bf16[4,128,128]{2,1,0:T(8,128)(2,1)S(1)}, u32[]{:S(2)}, u32[]{:S(2)}) collective-permute-start(bf16[4,128,128]{2,1,0:T(8,128)(2,1)S(1)} %bitcast.16), channel_id=1, source_target_pairs={{0,1},{1,0},{2,3},{3,2},{4,5},{5,4},{6,7},{7,6},{8,9},{9,8},{10,11... | collective-permute-start | bytes 393224 | tf_op jit(solution)/shard_map/ppermute | solution.py:409
  62.3 1.0 collective-permute-done.other_ref
  63.3 0.4 second_stage.1
  63.7 15.8 %all-gather = bf16[2048,128]{1,0:T(8,128)(2,1)S(1)} all-gather(bf16[256,128]{1,0:T(8,128)(2,1)S(1)} %second_stage.1), channel_id=2, replica_groups=mesh['dom'=64,'zh'=4,'core'=2] {'zh','core'}, dimensions={0}, use_global_device_ids=true | all-gather | bytes 589824 | tf_op jit(solution)/shard_map/all_gather | solution.py:411
  79.5 0.9 trace_stage.1
  80.3 0.1 broadcast_in_dim.8
  80.5 0.4 pad_maximum_fusion
  80.9 15.8 %all_to_all.17 = bf16[64,9,2,128]{3,2,1,0:T(2,128)(2,1)S(1)} all-to-all(bf16[64,9,2,128]{3,2,1,0:T(2,128)(2,1)S(1)} %pad_maximum_fusion), channel_id=1, replica_groups=mesh['dom'=64,'zh'=4,'core'=2] {'dom'}, dimensions={0} | all-to-all | bytes 589824 | tf_op jit(solution)/shard_map/all_to_all | solution.py:421
  96.7 3.7 %collective-permute-start.1 = (bf16[64,9,2,128]{3,2,1,0:T(2,128)(2,1)S(1)}, bf16[64,9,2,128]{3,2,1,0:T(2,128)(2,1)S(1)}, u32[]{:S(2)}, u32[]{:S(2)}) collective-permute-start(bf16[64,9,2,128]{3,2,1,0:T(2,128)(2,1)S(1)} %all_to_all.17), channel_id=1, source_target_pairs={{0,1},{1,0},{2,3},{3,2},{4,5},{5,4},{6,7},{7,6},{8,9},{9,8},{10,11... | collective-permute-start | bytes 884744 | tf_op jit(solution)/shard_map/ppermute | solution.py:422
  100.4 0.9 near_stage.1.base_ref
  101.3 0.3 collective-permute-done.1
  101.6 1.0 far_stage.1
Async XLA Ops:
  57.5 5.8 %collective-permute-start = (bf16[4,128,128]{2,1,0:T(8,128)(2,1)S(1)}, bf16[4,128,128]{2,1,0:T(8,128)(2,1)S(1)}, u32[]{:S(2)}, u32[]{:S(2)}) collective-permute-start(bf16[4,128,128]{2,1,0:T(8,128)(2,1)S(1)} %bitcast.16), channel_id=1, source_target_pairs={{0,1},{1,0},{2,3},{3,2},{4,5},{5,4},{6,7},{7,6},{8,9},{9,8},{10,11... | collective-permute-start | bytes 393224 | tf_op jit(solution)/shard_map/ppermute | solution.py:409
  96.7 4.9 %collective-permute-start.1 = (bf16[64,9,2,128]{3,2,1,0:T(2,128)(2,1)S(1)}, bf16[64,9,2,128]{3,2,1,0:T(2,128)(2,1)S(1)}, u32[]{:S(2)}, u32[]{:S(2)}) collective-permute-start(bf16[64,9,2,128]{3,2,1,0:T(2,128)(2,1)S(1)} %all_to_all.17), channel_id=1, source_target_pairs={{0,1},{1,0},{2,3},{3,2},{4,5},{5,4},{6,7},{7,6},{8,9},{9,8},{10,11... | collective-permute-start | bytes 884744 | tf_op jit(solution)/shard_map/ppermute | solution.py:422

commit v7 on v4

--- a/solution.py
+++ b/solution.py
@@ -60,9 +60,10 @@
                 (coup_hbm, coup_in),
                 (rows_hbm, rows_ref),
                 (colloc_hbm, colloc_ref),
+                (loads_hbm, loads_ref),
+                (inv_hbm.at[:, :LIVE], inv_ref.at[:, :LIVE]),
                 (factor_hbm, factor_ref),
-                (loads_hbm, loads_ref),
-                (inv_hbm, inv_ref),
+                (inv_hbm.at[:, LIVE:], inv_ref.at[:, LIVE:]),
                 (map_hbm, map_ref),
             ]
         )
@@ -99,12 +100,7 @@
     spots = turned(unit, spots)
     spots_ref[...] = spots + pltpu.roll(spots, LANE - 8, 1) + pltpu.roll(spots, LANE - 16, 1)
     landing_ref[...] = (iota((doms, doms), 0) == rows_ref[0, 0]).astype(BF16)
-    moves[7].wait()
-    for h in range(doms):
-        tile = factor_ref[pl.ds(16 * (h // 16), 16), pl.ds(LANE * (h % 16), LANE)]
-        sent_ref[ROWS * h : ROWS * h + 16, :] = tile.astype(BF16)
-    low_ref[...] = factor_ref[...].astype(BF16)
-    for move in moves[8:10]:
+    for move in moves[7:9]:
         move.wait()
     first = jnp.dot(inv_ref[0, :LIVE, :], loads_ref[0], preferred_element_type=F32)
     first_ref[...] = jnp.where(iota((LIVE, LANE), 0) < count, first, 0.0)
@@ -112,7 +108,13 @@
     row_ref[pl.ds(1, doms, stride=4), :] = first_ref[pl.ds(1, doms, stride=2), :]
     for h in range(doms):
         sent_ref[ROWS * h + 16 : ROWS * h + 20, :] = row_ref[4 * h : 4 * h + 4, :].astype(BF16)
-    moves[10].wait()
+    moves[9].wait()
+    for h in range(doms):
+        tile = factor_ref[pl.ds(16 * (h // 16), 16), pl.ds(LANE * (h % 16), LANE)]
+        sent_ref[ROWS * h : ROWS * h + 16, :] = tile.astype(BF16)
+    low_ref[...] = factor_ref[...].astype(BF16)
+    for move in moves[10:]:
+        move.wait()
 
 
 def first_stage(
@@ -148,7 +150,7 @@
             pltpu.VMEM((8, doms), F32),
             pltpu.VMEM((LIVE, LANE), F32),
             pltpu.VMEM((4 * doms, LANE), F32),
-            pltpu.SemaphoreType.DMA((11,)),
+            pltpu.SemaphoreType.DMA((12,)),
         ],
         compiler_params=PARAMS,
         name="first_stage",
@@ -163,7 +165,7 @@
     )
 
 
-def mix_kernel(got_ref, pair_ref, block_hbm, sent_ref, picks_ref, block_ref, row_ref, sem):
+def mix_kernel(got_ref, pair_ref, block_hbm, sent_ref, picks_ref, lane_ref, block_ref, row_ref, sem):
     doms = pair_ref.shape[0]
     cols = sent_ref.shape[0]
     move = pltpu.make_async_copy(block_hbm, block_ref, sem.at[0])
@@ -198,6 +200,7 @@
     for p in range(NPAN):
         owner = lax.div(block_ref[p], cols)
         picks_ref[p] = pair_ref[pl.ds(owner, 1)][0]
+        lane_ref[p] = jnp.full((8, LANE), lax.rem(block_ref[p], cols), jnp.int32)
 
 
 def mix_stage(got, panel_block, doms, cols):
@@ -206,9 +209,10 @@
         out_shape=(
             jax.ShapeDtypeStruct((cols, 2 * doms, LANE), BF16),
             jax.ShapeDtypeStruct((NPAN, ROWS // 2, 2, LANE), BF16),
+            jax.ShapeDtypeStruct((NPAN, 8, LANE), jnp.int32),
         ),
         in_specs=[VM, VM, pl.BlockSpec(memory_space=pltpu.HBM)],
-        out_specs=(VM, VM),
+        out_specs=(VM, VM, VM),
         scratch_shapes=[
             pltpu.SMEM(panel_block.shape, jnp.int32),
             pltpu.VMEM((4 * doms, LANE), F32),
@@ -250,52 +254,45 @@
     )(correction, loads, inverse, picks.reshape(NPAN * ROWS, LANE))
 
 
-def trace_kernel(
-    gathered_ref, map_ref, block_hbm, shared_ref, last_ref, block_ref, second_ref, row_ref, sem
-):
-    move = pltpu.make_async_copy(block_hbm, block_ref, sem.at[0])
-    move.start()
+def trace_kernel(gathered_ref, map_ref, lane_ref, sent_ref, second_ref, row_ref):
     cols = gathered_ref.shape[0]
     doms = map_ref.shape[1]
-    core = lax.rem(lax.axis_index("col"), 2)
+    first_core = lax.rem(lax.axis_index("col"), 2) == 0
+    lanes = [lane_ref[p][:1, :] for p in range(NPAN)]
+    chunk = jnp.zeros((16, LANE), F32)
+    quads = [jnp.zeros((1, LANE), F32)] * NPAN
     for c in range(cols):
         second_ref[MB * c : MB * (c + 1), :] = gathered_ref[c, :MB, :]
-    traces = jnp.dot(map_ref[0], second_ref[...], preferred_element_type=F32)
-    move.wait()
-    lanes = [lax.rem(block_ref[p], cols) for p in range(NPAN)]
-    own = jnp.where(core == 0, lanes[0], lanes[1])
-    first = gathered_ref[pl.ds(own, 1)][0, MB : MB + 16, :]
-    second = gathered_ref[pl.ds(own, 1)][0, MB + 16 : MB + 32, :]
-    shared_ref[...] = jnp.where(core == 0, first.astype(F32), second.astype(F32)).astype(BF16)
-    quads = [
-        gathered_ref[pl.ds(lanes[p], 1)][0, MB + 32 : MB + 48, :].astype(F32)[2 * p : 2 * p + 1, :]
-        for p in range(NPAN)
-    ]
+        rest = gathered_ref[c, MB : MB + 48, :].astype(F32)
+        tile = jnp.where(first_core, rest[:16], rest[16:32])
+        chunk = jnp.where(jnp.where(first_core, lanes[0], lanes[1]) == c, tile, chunk)
+        for p in range(NPAN):
+            quads[p] = jnp.where(lanes[p] == c, rest[32 + 2 * p : 33 + 2 * p], quads[p])
     tail = jnp.where(iota((1, LANE), 1) < 48, quads[0], pltpu.roll(quads[1], 48, 1))
-    row_ref[pl.ds(0, doms, stride=2), :] = traces
     row_ref[pl.ds(1, doms, stride=2), :] = jnp.broadcast_to(tail, (doms, LANE))
-    last_ref[...] = row_ref[...].astype(BF16)
-
-
-def trace_stage(gathered, trace_map, panel_block):
+    row_ref[pl.ds(0, doms, stride=2), :] = jnp.dot(
+        map_ref[0], second_ref[...], preferred_element_type=F32
+    )
+    chunk = chunk.astype(BF16)
+    for h in range(doms):
+        sent_ref[18 * h : 18 * h + 16, :] = chunk
+        sent_ref[18 * h + 16 : 18 * h + 18, :] = row_ref[2 * h : 2 * h + 2, :].astype(BF16)
+
+
+def trace_stage(gathered, trace_map, lanes):
     doms = trace_map.shape[1]
     return pl.pallas_call(
         trace_kernel,
-        out_shape=(
-            jax.ShapeDtypeStruct((16, LANE), BF16),
-            jax.ShapeDtypeStruct((2 * doms, LANE), BF16),
-        ),
-        in_specs=[VM, VM, pl.BlockSpec(memory_space=pltpu.HBM)],
-        out_specs=(VM, VM),
+        out_shape=jax.ShapeDtypeStruct((18 * doms, LANE), BF16),
+        in_specs=[VM, VM, VM],
+        out_specs=VM,
         scratch_shapes=[
-            pltpu.SMEM(panel_block.shape, jnp.int32),
             pltpu.VMEM((trace_map.shape[2], LANE), BF16),
             pltpu.VMEM((2 * doms, LANE), F32),
-            pltpu.SemaphoreType.DMA((1,)),
         ],
         compiler_params=PARAMS,
         name="trace_stage",
-    )(gathered, trace_map, pltpu.with_memory_space_constraint(panel_block, pltpu.HBM))
+    )(gathered, trace_map, lanes)
 
 
 def panel_of(block_ref, panel_ref, doms):
@@ -397,22 +394,15 @@
         colloc, quad_points, quad_weight, doms,
     )
     got = lax.all_to_all(sent.reshape(doms, ROWS // 2, 2, LANE), "dom", 0, 0, tiled=True)
-    sent, picks = mix_stage(got, panel_block, doms, cols)
+    sent, picks, lanes = mix_stage(got, panel_block, doms, cols)
 
     sent = sent.reshape(cols * doms, 2, LANE)
     correction = lax.all_to_all(sent, ("col", "dom"), 0, 0, tiled=True)
     correction = correction.reshape(cols, 2 * doms, LANE)
     pieces = second_stage(correction, loads, inverse, picks)
     gathered = lax.all_gather(pieces, "col", axis=0, tiled=False)
-    shared, last = trace_stage(gathered, trace_map, panel_block)
-
-    sent = jnp.concatenate(
-        [
-            jnp.broadcast_to(shared.reshape(1, 8, 2, LANE), (doms, 8, 2, LANE)),
-            last.reshape(doms, 1, 2, LANE),
-        ],
-        axis=1,
-    )
+
+    sent = trace_stage(gathered, trace_map, lanes).reshape(doms, 9, 2, LANE)
     got = lax.all_to_all(sent, "dom", 0, 0, tiled=True)
     other = lax.ppermute(got, "col", [(c, c ^ 1) for c in range(cols)])
     base = near_stage(got.reshape(18 * doms, LANE), factor_low, landing, spots)

time: 102 us -> 100 us (0.980)
  no operation moved by 1% of the time
where the time goes in v7:
time: 100 us
  blocking collectives  90.9 us (91%)
  Pallas kernels  4.96 us (5%)
  starting transfers between devices  3.98 us (4%)
    all_to_all x1, blocking collectives, local(): correction = lax.all_to_all(sent, ('col', 'dom'), 0, 0, tiled=True)  33.4 us
    all_to_all x1, blocking collectives, local(): lax.all_to_all(sent.reshape(doms, ROWS // 2, 2, LANE), 'dom', 0, 0, tiled...  24.6 us
    all_to_all x1, blocking collectives, local(): got = lax.all_to_all(sent, 'dom', 0, 0, tiled=True)  16.6 us
    all_gather x1, blocking collectives, local(): gathered = lax.all_gather(pieces, 'col', axis=0, tiled=False)  16.3 us
    ppermute x1, starting transfers between devices, local(): other = lax.ppermute(got, 'col', [(c, c ^ 1) for c in range(cols)])  3.98 us
  transfers between devices with their start and end apart: 1, of which 1 were waited for; matrix products, arithmetic and copies ran while one was open for 0% of the time, Pallas kernels for 1%

profile of v7, /device:TPU:1, one launch (start us, length us, event | category | flops | bytes accessed | tf_op | source)
XLA Modules:
  0.0 100.1 jit_solution(15190338846305045688)
XLA Ops:
  0.0 1.7 %first_stage.1 = (bf16[1280,128]{1,0:T(8,128)(2,1)S(1)}, bf16[1,208,1664]{2,1,0:T(8,128)(2,1)S(1)}, bf16[1,64,1664]{2,1,0:T(8,128)(2,1)S(1)}, bf16[1,1664,128]{2...) custom-call(bf16[1,208,1664]{2,1,0:T(8,128)(2,1)} %inv_hbm.1, ...), custom_call_target="tpu_custom_call" | custom-call | tf_op jit(solution)/shard_map/first_stage/pallas_call | solution.py:126
  1.7 24.6 %all_to_all.15.pair_ref = bf16[64,10,2,128]{3,2,1,0:T(2,128)(2,1)S(1)} all-to-all(bf16[64,10,2,128]{3,2,1,0:T(2,128)(2,1)S(1)} %bitcast.15), channel_id=1, replica_groups=mesh['dom'=64,'col'=8] {'dom'}, dimensions={0} | all-to-all | bytes 655360 | tf_op jit(solution)/shard_map/all_to_all | solution.py:396
  26.4 0.7 mix_stage.1
  27.1 33.4 %all_to_all.16 = bf16[512,2,128]{2,1,0:T(2,128)(2,1)S(1)} all-to-all(bf16[512,2,128]{2,1,0:T(2,128)(2,1)S(1)} %bitcast.17), channel_id=1, replica_groups=mesh['dom'=64,'col'=8] {'col','dom'}, dimensions={0} | all-to-all | bytes 524288 | tf_op jit(solution)/shard_map/all_to_all | solution.py:400
  60.5 0.4 second_stage.1
  60.9 16.3 %all-gather = bf16[2048,128]{1,0:T(8,128)(2,1)S(1)} all-gather(bf16[256,128]{1,0:T(8,128)(2,1)S(1)} %second_stage.1), channel_id=2, replica_groups=mesh['dom'=64,'col'=8] {'col'}, dimensions={0}, use_global_device_ids=true | all-gather | bytes 589824 | tf_op jit(solution)/shard_map/all_gather | solution.py:403
  77.2 0.3 trace_stage.1
  77.4 16.6 %all_to_all.17 = bf16[64,9,2,128]{3,2,1,0:T(2,128)(2,1)S(1)} all-to-all(bf16[64,9,2,128]{3,2,1,0:T(2,128)(2,1)S(1)} %bitcast.13), channel_id=1, replica_groups=mesh['dom'=64,'col'=8] {'dom'}, dimensions={0} | all-to-all | bytes 589824 | tf_op jit(solution)/shard_map/all_to_all | solution.py:406
  94.0 4.0 %collective-permute-start = (bf16[64,9,2,128]{3,2,1,0:T(2,128)(2,1)S(1)}, bf16[64,9,2,128]{3,2,1,0:T(2,128)(2,1)S(1)}, u32[]{:S(2)}, u32[]{:S(2)}) collective-permute-start(bf16[64,9,2,128]{3,2,1,0:T(2,128)(2,1)S(1)} %all_to_all.17), channel_id=1, source_target_pairs={{0,1},{1,0},{2,3},{3,2},{4,5},{5,4},{6,7},{7,6},{8,9},{9,8},{10,11... | collective-permute-start | bytes 884744 | tf_op jit(solution)/shard_map/ppermute | solution.py:407
  98.0 0.9 near_stage.1.base_ref
  98.9 0.3 collective-permute-done
  99.2 1.0 far_stage.1
Async XLA Ops:
  94.0 5.2 %collective-permute-start = (bf16[64,9,2,128]{3,2,1,0:T(2,128)(2,1)S(1)}, bf16[64,9,2,128]{3,2,1,0:T(2,128)(2,1)S(1)}, u32[]{:S(2)}, u32[]{:S(2)}) collective-permute-start(bf16[64,9,2,128]{3,2,1,0:T(2,128)(2,1)S(1)} %all_to_all.17), channel_id=1, source_target_pairs={{0,1},{1,0},{2,3},{3,2},{4,5},{5,4},{6,7},{7,6},{8,9},{9,8},{10,11... | collective-permute-start | bytes 884744 | tf_op jit(solution)/shard_map/ppermute | solution.py:407

commit v8 on v7

--- a/solution.py
+++ b/solution.py
@@ -42,9 +42,9 @@
 
 
 def first_kernel(
-    inv_hbm, map_hbm, loads_hbm, coup_hbm, listed_hbm, count_hbm, rows_hbm, factor_hbm, colloc_hbm,
+    inv_hbm, loads_hbm, coup_hbm, listed_hbm, count_hbm, rows_hbm, factor_hbm, colloc_hbm,
     points_hbm, weight_hbm,
-    sent_ref, inv_ref, map_ref, loads_ref, low_ref, landing_ref, spots_ref,
+    sent_ref, inv_ref, loads_ref, low_ref, landing_ref, spots_ref,
     coup_in, listed_ref, count_ref, rows_ref, factor_ref, colloc_ref, points_ref, weight_ref,
     quad_ref, coup_scr, spot_scr, first_ref, row_ref, sems,
 ):
@@ -61,10 +61,8 @@
                 (rows_hbm, rows_ref),
                 (colloc_hbm, colloc_ref),
                 (loads_hbm, loads_ref),
-                (inv_hbm.at[:, :LIVE], inv_ref.at[:, :LIVE]),
+                (inv_hbm.at[:, :LIVE], inv_ref),
                 (factor_hbm, factor_ref),
-                (inv_hbm.at[:, LIVE:], inv_ref.at[:, LIVE:]),
-                (map_hbm, map_ref),
             ]
         )
     ]
@@ -102,7 +100,7 @@
     landing_ref[...] = (iota((doms, doms), 0) == rows_ref[0, 0]).astype(BF16)
     for move in moves[7:9]:
         move.wait()
-    first = jnp.dot(inv_ref[0, :LIVE, :], loads_ref[0], preferred_element_type=F32)
+    first = jnp.dot(inv_ref[0], loads_ref[0], preferred_element_type=F32)
     first_ref[...] = jnp.where(iota((LIVE, LANE), 0) < count, first, 0.0)
     row_ref[pl.ds(0, doms, stride=4), :] = first_ref[pl.ds(0, doms, stride=2), :]
     row_ref[pl.ds(1, doms, stride=4), :] = first_ref[pl.ds(1, doms, stride=2), :]
@@ -113,12 +111,10 @@
         tile = factor_ref[pl.ds(16 * (h // 16), 16), pl.ds(LANE * (h % 16), LANE)]
         sent_ref[ROWS * h : ROWS * h + 16, :] = tile.astype(BF16)
     low_ref[...] = factor_ref[...].astype(BF16)
-    for move in moves[10:]:
-        move.wait()
 
 
 def first_stage(
-    inverse, trace_map, panel_coupling, coupling, neighbours, iface_count, surface_rows, factor,
+    inverse, panel_coupling, coupling, neighbours, iface_count, surface_rows, factor,
     colloc, quad_points, quad_weight, doms,
 ):
     shape = jax.ShapeDtypeStruct
@@ -127,15 +123,14 @@
         first_kernel,
         out_shape=(
             shape((ROWS * doms, LANE), BF16),
-            shape(inverse.shape, BF16),
-            shape(trace_map.shape, BF16),
+            shape((1, LIVE, inverse.shape[2]), BF16),
             shape(panel_coupling.shape, BF16),
             shape(factor.shape, BF16),
             shape((doms, doms), BF16),
             shape((doms, LANE), F32),
         ),
-        in_specs=[pl.BlockSpec(memory_space=pltpu.HBM)] * 11,
-        out_specs=(VM,) * 7,
+        in_specs=[pl.BlockSpec(memory_space=pltpu.HBM)] * 10,
+        out_specs=(VM,) * 6,
         scratch_shapes=[
             pltpu.VMEM(coupling.shape, F32),
             pltpu.SMEM(neighbours.shape, jnp.int32),
@@ -150,7 +145,7 @@
             pltpu.VMEM((8, doms), F32),
             pltpu.VMEM((LIVE, LANE), F32),
             pltpu.VMEM((4 * doms, LANE), F32),
-            pltpu.SemaphoreType.DMA((12,)),
+            pltpu.SemaphoreType.DMA((10,)),
         ],
         compiler_params=PARAMS,
         name="first_stage",
@@ -158,18 +153,24 @@
         *(
             pltpu.with_memory_space_constraint(x, pltpu.HBM)
             for x in (
-                inverse, trace_map, panel_coupling, coupling, neighbours, iface_count, surface_rows,
+                inverse, panel_coupling, coupling, neighbours, iface_count, surface_rows,
                 factor, colloc, quad_points, quad_weight,
             )
         )
     )
 
 
-def mix_kernel(got_ref, pair_ref, block_hbm, sent_ref, picks_ref, lane_ref, block_ref, row_ref, sem):
+def mix_kernel(
+    got_ref, pair_ref, block_hbm, inv_hbm, map_hbm, sent_ref, picks_ref, lane_ref, rest_ref, map_ref, block_ref, row_ref, sem
+):
     doms = pair_ref.shape[0]
     cols = sent_ref.shape[0]
     move = pltpu.make_async_copy(block_hbm, block_ref, sem.at[0])
     move.start()
+    rest = pltpu.make_async_copy(inv_hbm.at[:, LIVE:], rest_ref, sem.at[1])
+    rest.start()
+    maps = pltpu.make_async_copy(map_hbm, map_ref, sem.at[2])
+    maps.start()
     for h in range(doms):
         row_ref[4 * h : 4 * h + 4, :] = got_ref[ROWS * h + 16 : ROWS * h + 20, :].astype(F32)
     misc = row_ref[pl.ds(2, doms, stride=4), :]
@@ -201,22 +202,26 @@
         owner = lax.div(block_ref[p], cols)
         picks_ref[p] = pair_ref[pl.ds(owner, 1)][0]
         lane_ref[p] = jnp.full((8, LANE), lax.rem(block_ref[p], cols), jnp.int32)
-
-
-def mix_stage(got, panel_block, doms, cols):
+    rest.wait()
+    maps.wait()
+
+
+def mix_stage(got, panel_block, inverse, trace_map, doms, cols):
     return pl.pallas_call(
         mix_kernel,
         out_shape=(
             jax.ShapeDtypeStruct((cols, 2 * doms, LANE), BF16),
             jax.ShapeDtypeStruct((NPAN, ROWS // 2, 2, LANE), BF16),
             jax.ShapeDtypeStruct((NPAN, 8, LANE), jnp.int32),
+            jax.ShapeDtypeStruct((1, MB - LIVE, inverse.shape[2]), BF16),
+            jax.ShapeDtypeStruct(trace_map.shape, BF16),
         ),
-        in_specs=[VM, VM, pl.BlockSpec(memory_space=pltpu.HBM)],
-        out_specs=(VM, VM, VM),
+        in_specs=[VM, VM] + [pl.BlockSpec(memory_space=pltpu.HBM)] * 3,
+        out_specs=(VM,) * 5,
         scratch_shapes=[
             pltpu.SMEM(panel_block.shape, jnp.int32),
             pltpu.VMEM((4 * doms, LANE), F32),
-            pltpu.SemaphoreType.DMA((1,)),
+            pltpu.SemaphoreType.DMA((3,)),
         ],
         compiler_params=PARAMS,
         name="mix_stage",
@@ -224,34 +229,38 @@
         got.reshape(ROWS * doms, LANE),
         got,
         pltpu.with_memory_space_constraint(panel_block, pltpu.HBM),
-    )
-
-
-def second_kernel(correction_ref, loads_ref, inv_ref, picks_ref, out_ref, loaded_ref):
+        pltpu.with_memory_space_constraint(inverse, pltpu.HBM),
+        pltpu.with_memory_space_constraint(trace_map, pltpu.HBM),
+    )
+
+
+def second_kernel(correction_ref, loads_ref, inv_ref, rest_ref, picks_ref, out_ref, loaded_ref):
     cols = correction_ref.shape[0]
     for c in range(cols):
         top = loads_ref[0, MB * c : MB * c + MAX_LIVE, :].astype(F32)
         top = top - correction_ref[c, :MAX_LIVE, :].astype(F32)
         loaded_ref[MB * c : MB * c + MAX_LIVE, :] = top.astype(BF16)
         loaded_ref[MB * c + MAX_LIVE : MB * (c + 1), :] = loads_ref[0, MB * c + MAX_LIVE : MB * (c + 1), :]
-    second = jnp.dot(inv_ref[0], loaded_ref[...], preferred_element_type=F32)
-    out_ref[:MB, :] = second.astype(BF16)
+    top = jnp.dot(inv_ref[0], loaded_ref[...], preferred_element_type=F32)
+    out_ref[:LIVE, :] = top.astype(BF16)
+    bottom = jnp.dot(rest_ref[0], loaded_ref[...], preferred_element_type=F32)
+    out_ref[LIVE:MB, :] = bottom.astype(BF16)
     out_ref[MB + 32 :, :] = jnp.zeros((16, LANE), BF16)
     for p in range(NPAN):
         out_ref[MB + 16 * p : MB + 16 * p + 16, :] = picks_ref[ROWS * p : ROWS * p + 16, :]
         out_ref[MB + 32 + 2 * p : MB + 34 + 2 * p, :] = picks_ref[ROWS * p + 18 : ROWS * p + 20, :]
 
 
-def second_stage(correction, loads, inverse, picks):
+def second_stage(correction, loads, inverse, rest, picks):
     return pl.pallas_call(
         second_kernel,
         out_shape=jax.ShapeDtypeStruct((MB + 48, LANE), BF16),
-        in_specs=[VM] * 4,
+        in_specs=[VM] * 5,
         out_specs=VM,
         scratch_shapes=[pltpu.VMEM(loads.shape[1:], BF16)],
         compiler_params=PARAMS,
         name="second_stage",
-    )(correction, loads, inverse, picks.reshape(NPAN * ROWS, LANE))
+    )(correction, loads, inverse, rest, picks.reshape(NPAN * ROWS, LANE))
 
 
 def trace_kernel(gathered_ref, map_ref, lane_ref, sent_ref, second_ref, row_ref):
@@ -389,17 +398,19 @@
 ):
     doms = lax.axis_size("dom")
     cols = lax.axis_size("col")
-    sent, inverse, trace_map, loads, factor_low, landing, spots = first_stage(
-        inverse, trace_map, panel_coupling, coupling, neighbours, iface_count, surface_rows, factor,
+    sent, top, loads, factor_low, landing, spots = first_stage(
+        inverse, panel_coupling, coupling, neighbours, iface_count, surface_rows, factor,
         colloc, quad_points, quad_weight, doms,
     )
     got = lax.all_to_all(sent.reshape(doms, ROWS // 2, 2, LANE), "dom", 0, 0, tiled=True)
-    sent, picks, lanes = mix_stage(got, panel_block, doms, cols)
+    sent, picks, lanes, rest, trace_map = mix_stage(
+        got, panel_block, inverse, trace_map, doms, cols
+    )
 
     sent = sent.reshape(cols * doms, 2, LANE)
     correction = lax.all_to_all(sent, ("col", "dom"), 0, 0, tiled=True)
     correction = correction.reshape(cols, 2 * doms, LANE)
-    pieces = second_stage(correction, loads, inverse, picks)
+    pieces = second_stage(correction, loads, top, rest, picks)
     gathered = lax.all_gather(pieces, "col", axis=0, tiled=False)
 
     sent = trace_stage(gathered, trace_map, lanes).reshape(doms, 9, 2, LANE)

time: 100 us -> 101 us (1.010)
  no operation moved by 1% of the time
where the time goes in v8:
time: 101 us; the launch traced here: 100 us
  blocking collectives  90.9 us (90%)
  Pallas kernels  5.27 us (5%)
  starting transfers between devices  3.98 us (4%)
    all_to_all x1, blocking collectives, local(): correction = lax.all_to_all(sent, ('col', 'dom'), 0, 0, tiled=True)  33.4 us
    all_to_all x1, blocking collectives, local(): lax.all_to_all(sent.reshape(doms, ROWS // 2, 2, LANE), 'dom', 0, 0, tiled...  24.7 us
    all_to_all x1, blocking collectives, local(): got = lax.all_to_all(sent, 'dom', 0, 0, tiled=True)  16.6 us
    all_gather x1, blocking collectives, local(): gathered = lax.all_gather(pieces, 'col', axis=0, tiled=False)  16.3 us
    ppermute x1, starting transfers between devices, local(): other = lax.ppermute(got, 'col', [(c, c ^ 1) for c in range(cols)])  3.98 us
  transfers between devices with their start and end apart: 1, of which 1 were waited for; matrix products, arithmetic and copies ran while one was open for 0% of the time, Pallas kernels for 1%

profile of v8, /device:TPU:1, one launch (start us, length us, event | category | flops | bytes accessed | tf_op | source)
XLA Modules:
  0.0 100.5 jit_solution(153799386359778053)
XLA Ops:
  0.0 1.7 %first_stage.1 = (bf16[1280,128]{1,0:T(8,128)(2,1)S(1)}, bf16[1,128,1664]{2,1,0:T(8,128)(2,1)S(1)}, bf16[1,1664,128]{2,1,0:T(8,128)(2,1)S(1)}, bf16[64,2048]{1,0...) custom-call(bf16[1,208,1664]{2,1,0:T(8,128)(2,1)} %inv_hbm.3, bf16[1,1664,128]{2,1,0:T(8,128)(2,1)} %loads_hbm.1, ...), custom_call_target="tpu_custom_call" | custom-call | tf_op jit(solution)/shard_map/first_stage/pallas_call | solution.py:122
  1.7 24.7 %all_to_all.15.pair_ref = bf16[64,10,2,128]{3,2,1,0:T(2,128)(2,1)S(1)} all-to-all(bf16[64,10,2,128]{3,2,1,0:T(2,128)(2,1)S(1)} %bitcast.15), channel_id=1, replica_groups=mesh['dom'=64,'col'=8] {'dom'}, dimensions={0} | all-to-all | bytes 655360 | tf_op jit(solution)/shard_map/all_to_all | solution.py:405
  26.4 1.1 %mix_stage.1 = (bf16[8,128,128]{2,1,0:T(8,128)(2,1)S(1)}, bf16[2,10,2,128]{3,2,1,0:T(2,128)(2,1)S(1)}, s32[2,8,128]{2,1,0:T(8,128)S(1)}, bf16[1,80,1664]{2,1,0:T(8,128)(2,1)S(1)}, bf16[1,64,1664]{2,1,0:T(8,128)(2,1)S(1)}) custom-call(bf16[1280,128]{1,0:T(8,128)(2,1)S(1)} %bitcast.10, bf16[64,10,2,128]{3,2,1,0:T(2,128)(2,1)S(1)} %all_to_all.15.pair_ref, ...), custom_call_target="tpu_custom_call" | custom-call | tf_op jit(solution)/shard_map/mix_stage/pallas_call | solution.py:210
  27.5 33.4 %all_to_all.16 = bf16[512,2,128]{2,1,0:T(2,128)(2,1)S(1)} all-to-all(bf16[512,2,128]{2,1,0:T(2,128)(2,1)S(1)} %bitcast.17), channel_id=1, replica_groups=mesh['dom'=64,'col'=8] {'col','dom'}, dimensions={0} | all-to-all | bytes 524288 | tf_op jit(solution)/shard_map/all_to_all | solution.py:411
  60.8 0.4 second_stage.1
  61.2 16.3 %all-gather = bf16[2048,128]{1,0:T(8,128)(2,1)S(1)} all-gather(bf16[256,128]{1,0:T(8,128)(2,1)S(1)} %second_stage.1), channel_id=2, replica_groups=mesh['dom'=64,'col'=8] {'col'}, dimensions={0}, use_global_device_ids=true | all-gather | bytes 589824 | tf_op jit(solution)/shard_map/all_gather | solution.py:414
  77.5 0.3 trace_stage.1
  77.7 16.6 %all_to_all.17 = bf16[64,9,2,128]{3,2,1,0:T(2,128)(2,1)S(1)} all-to-all(bf16[64,9,2,128]{3,2,1,0:T(2,128)(2,1)S(1)} %bitcast.13), channel_id=1, replica_groups=mesh['dom'=64,'col'=8] {'dom'}, dimensions={0} | all-to-all | bytes 589824 | tf_op jit(solution)/shard_map/all_to_all | solution.py:417
  94.3 4.0 %collective-permute-start = (bf16[64,9,2,128]{3,2,1,0:T(2,128)(2,1)S(1)}, bf16[64,9,2,128]{3,2,1,0:T(2,128)(2,1)S(1)}, u32[]{:S(2)}, u32[]{:S(2)}) collective-permute-start(bf16[64,9,2,128]{3,2,1,0:T(2,128)(2,1)S(1)} %all_to_all.17), channel_id=1, source_target_pairs={{0,1},{1,0},{2,3},{3,2},{4,5},{5,4},{6,7},{7,6},{8,9},{9,8},{10,11... | collective-permute-start | bytes 884744 | tf_op jit(solution)/shard_map/ppermute | solution.py:418
  98.3 0.9 near_stage.1.base_ref
  99.2 0.3 collective-permute-done
  99.5 1.0 far_stage.1
Async XLA Ops:
  94.3 5.2 %collective-permute-start = (bf16[64,9,2,128]{3,2,1,0:T(2,128)(2,1)S(1)}, bf16[64,9,2,128]{3,2,1,0:T(2,128)(2,1)S(1)}, u32[]{:S(2)}, u32[]{:S(2)}) collective-permute-start(bf16[64,9,2,128]{3,2,1,0:T(2,128)(2,1)S(1)} %all_to_all.17), channel_id=1, source_target_pairs={{0,1},{1,0},{2,3},{3,2},{4,5},{5,4},{6,7},{7,6},{8,9},{9,8},{10,11... | collective-permute-start | bytes 884744 | tf_op jit(solution)/shard_map/ppermute | solution.py:418

commit v9 on v7

--- a/solution.py
+++ b/solution.py
@@ -183,12 +183,10 @@
             mixing = mixing + jnp.where(
                 misc[:, 96 + k : 97 + k] == sources, weights[:, lane : lane + 1], 0.0
             )
-        summed = jnp.dot(
-            mixing,
-            row_ref[pl.ds(r, doms, stride=4), :],
-            precision=lax.Precision.HIGHEST,
-            preferred_element_type=F32,
-        )
+        values = row_ref[pl.ds(r, doms, stride=4), :].astype(BF16)
+        summed = jnp.zeros((doms, LANE), F32)
+        for term in reversed(terms(mixing)):
+            summed = summed + jnp.dot(term.astype(BF16), values, preferred_element_type=F32)
         row = (2 * lax.axis_index("dom") + r).astype(F32)
         mixed.append(jnp.where(misc[:, 102:103] > row, summed, 0.0))
     row_ref[pl.ds(0, doms, stride=2), :] = mixed[0]

time: 100 us -> 100 us (level)
  no operation moved by 1% of the time
where the time goes in v9:
time: 100 us
  blocking collectives  90.9 us (91%)
  Pallas kernels  4.96 us (5%)
  starting transfers between devices  3.98 us (4%)
    all_to_all x1, blocking collectives, local(): correction = lax.all_to_all(sent, ('col', 'dom'), 0, 0, tiled=True)  33.4 us
    all_to_all x1, blocking collectives, local(): lax.all_to_all(sent.reshape(doms, ROWS // 2, 2, LANE), 'dom', 0, 0, tiled...  24.6 us
    all_to_all x1, blocking collectives, local(): got = lax.all_to_all(sent, 'dom', 0, 0, tiled=True)  16.6 us
    all_gather x1, blocking collectives, local(): gathered = lax.all_gather(pieces, 'col', axis=0, tiled=False)  16.3 us
    ppermute x1, starting transfers between devices, local(): other = lax.ppermute(got, 'col', [(c, c ^ 1) for c in range(cols)])  3.98 us
  transfers between devices with their start and end apart: 1, of which 1 were waited for; matrix products, arithmetic and copies ran while one was open for 0% of the time, Pallas kernels for 1%

profile of v9, /device:TPU:1, one launch (start us, length us, event | category | flops | bytes accessed | tf_op | source)
XLA Modules:
  0.0 100.1 jit_solution(15759062947429124088)
XLA Ops:
  0.0 1.7 %first_stage.1 = (bf16[1280,128]{1,0:T(8,128)(2,1)S(1)}, bf16[1,208,1664]{2,1,0:T(8,128)(2,1)S(1)}, bf16[1,64,1664]{2,1,0:T(8,128)(2,1)S(1)}, bf16[1,1664,128]{2...) custom-call(bf16[1,208,1664]{2,1,0:T(8,128)(2,1)} %inv_hbm.1, ...), custom_call_target="tpu_custom_call" | custom-call | tf_op jit(solution)/shard_map/first_stage/pallas_call | solution.py:126
  1.7 24.6 %all_to_all.15.pair_ref = bf16[64,10,2,128]{3,2,1,0:T(2,128)(2,1)S(1)} all-to-all(bf16[64,10,2,128]{3,2,1,0:T(2,128)(2,1)S(1)} %bitcast.15), channel_id=1, replica_groups=mesh['dom'=64,'col'=8] {'dom'}, dimensions={0} | all-to-all | bytes 655360 | tf_op jit(solution)/shard_map/all_to_all | solution.py:394
  26.4 0.7 mix_stage.1
  27.1 33.4 %all_to_all.16 = bf16[512,2,128]{2,1,0:T(2,128)(2,1)S(1)} all-to-all(bf16[512,2,128]{2,1,0:T(2,128)(2,1)S(1)} %bitcast.17), channel_id=1, replica_groups=mesh['dom'=64,'col'=8] {'col','dom'}, dimensions={0} | all-to-all | bytes 524288 | tf_op jit(solution)/shard_map/all_to_all | solution.py:398
  60.5 0.4 second_stage.1
  60.9 16.3 %all-gather = bf16[2048,128]{1,0:T(8,128)(2,1)S(1)} all-gather(bf16[256,128]{1,0:T(8,128)(2,1)S(1)} %second_stage.1), channel_id=2, replica_groups=mesh['dom'=64,'col'=8] {'col'}, dimensions={0}, use_global_device_ids=true | all-gather | bytes 589824 | tf_op jit(solution)/shard_map/all_gather | solution.py:401
  77.2 0.3 trace_stage.1
  77.4 16.6 %all_to_all.17 = bf16[64,9,2,128]{3,2,1,0:T(2,128)(2,1)S(1)} all-to-all(bf16[64,9,2,128]{3,2,1,0:T(2,128)(2,1)S(1)} %bitcast.13), channel_id=1, replica_groups=mesh['dom'=64,'col'=8] {'dom'}, dimensions={0} | all-to-all | bytes 589824 | tf_op jit(solution)/shard_map/all_to_all | solution.py:404
  94.0 4.0 %collective-permute-start = (bf16[64,9,2,128]{3,2,1,0:T(2,128)(2,1)S(1)}, bf16[64,9,2,128]{3,2,1,0:T(2,128)(2,1)S(1)}, u32[]{:S(2)}, u32[]{:S(2)}) collective-permute-start(bf16[64,9,2,128]{3,2,1,0:T(2,128)(2,1)S(1)} %all_to_all.17), channel_id=1, source_target_pairs={{0,1},{1,0},{2,3},{3,2},{4,5},{5,4},{6,7},{7,6},{8,9},{9,8},{10,11... | collective-permute-start | bytes 884744 | tf_op jit(solution)/shard_map/ppermute | solution.py:405
  98.0 0.9 near_stage.1.base_ref
  98.9 0.3 collective-permute-done
  99.2 1.0 far_stage.1
Async XLA Ops:
  94.0 5.2 %collective-permute-start = (bf16[64,9,2,128]{3,2,1,0:T(2,128)(2,1)S(1)}, bf16[64,9,2,128]{3,2,1,0:T(2,128)(2,1)S(1)}, u32[]{:S(2)}, u32[]{:S(2)}) collective-permute-start(bf16[64,9,2,128]{3,2,1,0:T(2,128)(2,1)S(1)} %all_to_all.17), channel_id=1, source_target_pairs={{0,1},{1,0},{2,3},{3,2},{4,5},{5,4},{6,7},{7,6},{8,9},{9,8},{10,11... | collective-permute-start | bytes 884744 | tf_op jit(solution)/shard_map/ppermute | solution.py:405
